TPU v7x, 128 devices: a whole 4x4x4 slice. The times are simulated.
128 devices in a mesh: row: 4 (over y_lo, core), col: 32 (over y_hi, z, x).
Axes of the slice: x: 4, y: 4 (y_hi: 2, y_lo: 2; y = y_hi * 2 + y_lo), z: 4, core: 2. Of those that a mesh axis runs over, the one named last changes fastest.
Arguments:
- sky: bfloat16 [128, 1024, 4096], P(None, 'row', 'col'), may hold values from -80 to 80
- kernel_widths: int32 [2], replicated, may hold values from 16 to 32, as said below
- prior_var: float32 [2, 128], replicated, may hold values from 0.05 to 0.5
- tile_region: int32 [4, 32], P('row', 'col'), may hold values from 0 to 7, as said below
- region_rank: int32 [8], replicated, may hold values from 2 to 8
Outputs:
- cleaned: bfloat16 [128, 1024, 4096], P(None, 'row', 'col')
Inputs may be any that keep to these rules, and one draw needn't show every extreme that they name: `kernel_widths`: entry 0 is the half-width along the sky's rows (second dimension of sky), entry 1 along its columns; one of the two equals 32, the other is below 32. `tile_region`: each region holds exactly 16 tiles, anywhere on the sky.
All inputs are finite; a program needn't handle non-finite values.
Results may differ from a plain program's by a relative error of at most 0.0085.
Values may be sent and summed in bfloat16 or wider, within the bound.
A program may use at most 128 MiB of HBM per device.

v0:
```python
import math

import jax
import jax.numpy as jnp
from jax import lax
from jax.sharding import PartitionSpec as P

HW = 32
MMAX = 8
TPR = 16


def extended_2(cells, sides, width):
    for axis, dim in sides:
        count = lax.axis_size(axis)
        ends = count - 1
        head = lax.slice_in_dim(cells, 0, width, axis=dim)
        tail = lax.slice_in_dim(cells, cells.shape[dim] - width, cells.shape[dim], axis=dim)
        cells = jnp.concatenate(
            [
                lax.ppermute(tail, axis, [(i, (i + 1) % count) for i in range(ends)]),
                cells,
                lax.ppermute(head, axis, [((i + 1) % count, i) for i in range(ends)]),
            ],
            axis=dim,
        )
    return cells


def raised(offsets, half_width):
    spread = half_width.astype(jnp.float32)
    inside = jnp.abs(offsets) <= spread
    values = (1.0 + jnp.cos(math.pi * offsets / (spread + 1.0))) / (2.0 * spread + 2.0)
    return jnp.where(inside, values, jnp.zeros_like(values))


def toeplitz(length, half_width):
    inputs = jnp.arange(length + 2 * HW, dtype=jnp.float32)[:, None]
    outputs = jnp.arange(length, dtype=jnp.float32)[None, :]
    offsets = inputs - outputs - HW
    return raised(offsets, half_width).astype(jnp.bfloat16)


def chebyshev(chan_count, degree):
    position = (2.0 * jnp.arange(chan_count, dtype=jnp.float32) + 1.0) / chan_count - 1.0
    terms = [jnp.ones_like(position), position]
    for order in range(2, degree):
        terms.append(2.0 * position * terms[-1] - terms[-2])
    return jnp.stack(terms[:degree], axis=1)


def spd_solve(matrix, right_hand):
    factor = jnp.linalg.cholesky(matrix)
    middle = lax.linalg.triangular_solve(factor, right_hand, left_side=True, lower=True)
    return lax.linalg.triangular_solve(factor, middle, left_side=True, lower=True, transpose_a=True)


def projector(gram_sum, prior_row, keep_rank, pixels):
    chan_count = gram_sum.shape[0]
    cheb_basis = chebyshev(chan_count, MMAX)
    covariance = gram_sum / pixels + jnp.diag(prior_row)
    mixed = spd_solve(covariance, cheb_basis)
    keep_mask = (jnp.arange(MMAX) < keep_rank).astype(jnp.float32)
    kept_basis = cheb_basis * keep_mask
    kept_mixed = mixed * keep_mask
    small_matrix = jnp.dot(kept_basis.T, kept_mixed, precision=lax.Precision.HIGHEST) + jnp.diag(
        1.0 - keep_mask
    )
    weights = spd_solve(small_matrix, kept_mixed.T)
    return jnp.dot(kept_basis, weights, precision=lax.Precision.HIGHEST).astype(jnp.bfloat16)


def local(sky, kernel_widths, prior_var, tile_region, region_rank):
    chan_count, tile_rows, tile_cols = sky.shape
    down_table = toeplitz(tile_rows, kernel_widths[0])
    across_table = toeplitz(tile_cols, kernel_widths[1])
    extended = extended_2(sky, (("row", 1), ("col", 2)), HW)
    smooth = jnp.einsum(
        "cyx,yz->czx", extended, down_table, preferred_element_type=jnp.float32
    ).astype(jnp.bfloat16)
    coarse = jnp.einsum(
        "cyx,xz->cyz", smooth, across_table, preferred_element_type=jnp.float32
    ).astype(jnp.bfloat16)
    fine = (sky.astype(jnp.float32) - coarse.astype(jnp.float32)).astype(jnp.bfloat16)
    coarse_gram = jnp.einsum("cyx,dyx->cd", coarse, coarse, preferred_element_type=jnp.float32)
    fine_gram = jnp.einsum("cyx,dyx->cd", fine, fine, preferred_element_type=jnp.float32)
    grams = jnp.stack([coarse_gram, fine_gram], axis=0)
    region = tile_region[0, 0]
    region_count = region_rank.shape[0]
    slot_mask = (jnp.arange(region_count) == region).astype(jnp.float32)
    slotted = slot_mask[:, None, None, None] * grams[None]
    totals = lax.psum(slotted, ("row", "col"))
    own_gram = lax.dynamic_index_in_dim(totals, region, 0, keepdims=False)
    keep_rank = lax.dynamic_index_in_dim(region_rank, region, 0, keepdims=False)
    pixels = TPR * tile_rows * tile_cols
    coarse_proj = projector(own_gram[0], prior_var[0], keep_rank, pixels)
    fine_proj = projector(own_gram[1], prior_var[1], keep_rank, pixels)
    removed = jnp.einsum("ij,jyx->iyx", coarse_proj, coarse, preferred_element_type=jnp.float32)
    removed = removed + jnp.einsum(
        "ij,jyx->iyx", fine_proj, fine, preferred_element_type=jnp.float32
    )
    cleaned = coarse.astype(jnp.float32) + fine.astype(jnp.float32) - removed
    return cleaned.astype(jnp.bfloat16)


def solution(mesh):
    return jax.shard_map(
        local,
        mesh=mesh,
        in_specs=(P(None, "row", "col"), P(), P(), P("row", "col"), P()),
        out_specs=P(None, "row", "col"),
        check_vma=False,
    )
```

profile of v0, /device:TPU:1, one launch (start us, length us, event | category | flops | bytes accessed | tf_op | source)
XLA Modules:
  0.0 505.3 jit_solution(14698396365791912761)
XLA Ops:
  6.5 12.7 %copy.25 = bf16[128,256,128]{0,2,1:T(8,128)(2,1)} copy(bf16[128,256,128]{2,1,0:T(8,128)(2,1)} %param.15) | data formatting | bytes 16777216 | tf_op args[0]
  20.9 4.6 collective-permute-start
  25.5 1.9 collective-permute-start.1
  27.4 9.8 %collective-permute-done = bf16[128,32,128]{0,2,1:T(8,128)(2,1)S(1)} collective-permute-done((bf16[128,32,128]{0,2,1:T(8,128)(2,1)S(1)}, bf16[128,32,128]{0,2,1:T(8,128)(2,1)S(1)}, u32[]{:S(2)}, u32[]{:S(2)}) %collective-permute-start) | collective-permute-done | bytes 1048608 | tf_op jit(solution)/shard_map/ppermute | solution.py:21
  37.2 4.4 collective-permute-done.1
  41.6 7.7 %pad_maximum_fusion.3 = (bf16[128,320,32]{0,2,1:T(8,128)(2,1)}, bf16[128,320,32]{0,2,1:T(8,128)(2,1)}) fusion(bf16[128,32,128]{0,2,1:T(8,128)(2,1)S(1)} %collective-permute-done.1, bf16[128,256,128]{0,2,1:T(8,128)(2,1)} %copy.25, bf16[128,32,128]{0,2,1:T(8,128)(2,1)S(1)} %collective-permute-done), kind=kLoop, calls=%fused_computation.18 | loop fusion | flops 15728640 | bytes 15728640 | tf_op jit(solution)/shard_map/slice | solution.py:18
  49.3 4.6 collective-permute-start.2
  58.7 39.6 %collective-permute-done.2 = bf16[128,320,32]{0,2,1:T(8,128)(2,1)} collective-permute-done((bf16[128,320,32]{0,2,1:T(8,128)(2,1)}, bf16[128,320,32]{0,2,1:T(8,128)(2,1)}, u32[]{:S(2)}, u32[]{:S(2)}) %collective-permute-start.2) | collective-permute-done | bytes 2621472 | tf_op jit(solution)/shard_map/ppermute | solution.py:21
  98.3 5.6 %collective-permute-done.3 = bf16[128,320,32]{0,2,1:T(8,128)(2,1)} collective-permute-done((bf16[128,320,32]{0,2,1:T(8,128)(2,1)}, bf16[128,320,32]{0,2,1:T(8,128)(2,1)}, u32[]{:S(2)}, u32[]{:S(2)}) %collective-permute-start.3) | collective-permute-done | bytes 2621472 | tf_op jit(solution)/shard_map/ppermute | solution.py:23
  103.9 29.0 %pad_maximum_fusion = bf16[128,320,192]{0,2,1:T(8,128)(2,1)} fusion(bf16[128,320,32]{0,2,1:T(8,128)(2,1)} %collective-permute-done.3, bf16[128,32,128]{0,2,1:T(8,128)(2,1)S(1)} %collective-permute-done.1, bf16[128,256,128]{0,2,1:T(8,128)(2,1)} %copy.25, bf16[128,32,128]{0,2,1:T(8,128)(2,1)S(1)} %collective-permute-done, ...), kind=kLoop, calls=%fused_computation.6 | loop fusion | flops 78643200 | bytes 31457280 | tf_op jit(solution)/shard_map/concatenate | solution.py:19
  133.0 26.4 %copy.47 = bf16[128,320,192]{1,2,0:T(8,128)(2,1)} copy(bf16[128,320,192]{0,2,1:T(8,128)(2,1)} %pad_maximum_fusion) | data formatting | bytes 31457280 | tf_op jit(solution)/shard_map/concatenate | solution.py:19
  159.3 25.8 %fusion = (bf16[128,256,128]{2,1,0:T(8,128)(2,1)}, bf16[128,256,128]{2,1,0:T(8,128)(2,1)}) fusion(bf16[128,256,128]{2,1,0:T(8,128)(2,1)} %param.15, f32[]{:T(128)S(6)} %add.184, f32[]{:T(128)S(6)} %add.181, f32[]{:T(128)} %bitcast.4, bf16[128,320,192]{1,2,0:T(8,128)(2,1)} %copy.47, f32[]{:T(128)S(6)} %add.180, f32[]{:T(128)S(6)} %add.177, f32[]{:T(128)} %bitcast.1), kind=kOutput, calls=%fused_computation.2 | convolution fusion | flops 5665472512 | bytes 40894488 | tf_op jit(solution)/shard_map/cyx,xz->cyz/dot_general | solution.py:81
  185.1 12.5 %copy.30 = bf16[128,256,128]{1,0,2:T(8,128)(2,1)} copy(bf16[128,256,128]{2,1,0:T(8,128)(2,1)} %get-tuple-element.21) | data formatting | bytes 16777216 | tf_op jit(solution)/shard_map/convert_element_type | solution.py:84
  197.7 8.1 %convolution_bitcast_fusion = f32[1,128,128]{2,1,0:T(8,128)S(1)} fusion(bf16[128,256,128]{1,0,2:T(8,128)(2,1)} %copy.30), kind=kOutput, calls=%fused_computation.19 | convolution fusion | flops 1073741824 | bytes 8454144 | tf_op jit(solution)/shard_map/cyx,dyx->cd/dot_general | solution.py:86
  205.8 12.9 %copy.28 = bf16[128,256,128]{1,0,2:T(8,128)(2,1)} copy(bf16[128,256,128]{2,1,0:T(8,128)(2,1)} %get-tuple-element.22) | data formatting | bytes 16777216 | tf_op jit(solution)/shard_map/convert_element_type | solution.py:83
  218.7 8.1 %convolution_bitcast_fusion.1 = f32[1,128,128]{2,1,0:T(8,128)S(1)} fusion(bf16[128,256,128]{1,0,2:T(8,128)(2,1)} %copy.28), kind=kOutput, calls=%fused_computation.20 | convolution fusion | flops 1073741824 | bytes 8454144 | tf_op jit(solution)/shard_map/cyx,dyx->cd/dot_general | solution.py:85
  229.5 150.2 %all-reduce.2.cloned.1.call-done = f32[8,2,128,128]{2,3,1,0:T(8,128)} async-done(((f32[8,2,128,128]{2,3,1,0:T(8,128)}), f32[8,2,128,128]{2,3,1,0:T(8,128)}) %all-reduce.2.cloned.1.call-update) | async-done | bytes 1048592 | tf_op jit(solution)/shard_map/psum | solution.py:92
  380.9 11.7 %cholesky.108 = f32[128,128]{1,0:T(8,128)S(1)} custom-call(f32[128,128]{1,0:T(8,128)S(1)} %get-tuple-element.29), custom_call_target="Cholesky" | custom-call | tf_op jit(solution)/shard_map/jit(cholesky)/cholesky | solution.py:53
  393.9 9.8 %custom-call.25 = f32[1,128,128]{1,2,0:T(8,128)S(1)} custom-call(f32[1,128,128]{2,1,0:T(8,128)S(1)} %fusion.35), custom_call_target="InvertDiagBlocksLowerTriangular" | custom-call | tf_op jit(solution)/shard_map/triangular_solve/custom-call.3 | solution.py:55
  403.7 11.7 %cholesky.86 = f32[128,128]{1,0:T(8,128)S(1)} custom-call(f32[128,128]{1,0:T(8,128)S(1)} %get-tuple-element.30), custom_call_target="Cholesky" | custom-call | tf_op jit(solution)/shard_map/jit(cholesky)/cholesky | solution.py:53
  416.8 10.0 %custom-call.21 = f32[1,128,128]{1,2,0:T(8,128)S(1)} custom-call(f32[1,128,128]{2,1,0:T(8,128)S(1)} %fusion.34), custom_call_target="InvertDiagBlocksLowerTriangular" | custom-call | tf_op jit(solution)/shard_map/triangular_solve/custom-call.3 | solution.py:55
  435.3 15.6 %fusion.8 = f32[128,256,128]{2,0,1:T(8,128)} fusion(bf16[128,128,1]{1,0,2:T(8,128)(2,1)S(1)} %fusion.16, bf16[128,256,128]{2,1,0:T(8,128)(2,1)} %get-tuple-element.21), kind=kOutput, calls=%fused_computation.11 | convolution fusion | flops 1073741824 | bytes 25198592 | tf_op jit(solution)/shard_map/ij,jyx->iyx/dot_general | solution.py:99
  450.8 15.8 %fusion.10 = f32[128,256,128]{2,0,1:T(8,128)} fusion(bf16[128,128,1]{1,0,2:T(8,128)(2,1)S(1)} %fusion.15, bf16[128,256,128]{2,1,0:T(8,128)(2,1)} %get-tuple-element.22), kind=kOutput, calls=%fused_computation.13 | convolution fusion | flops 1073741824 | bytes 25198592 | tf_op jit(solution)/shard_map/ij,jyx->iyx/dot_general | solution.py:98
  466.6 31.6 %fusion.2 = bf16[128,256,128]{2,1,0:T(8,128)(2,1)} fusion(bf16[128,256,128]{2,1,0:T(8,128)(2,1)S(1)} %bitcast.129, f32[128,256,128]{2,0,1:T(8,128)} %fusion.8, f32[128,256,128]{2,0,1:T(8,128)} %fusion.10, bf16[128,256,128]{2,1,0:T(8,128)(2,1)S(1)} %bitcast.131), kind=kLoop, calls=%fused_computation.4 | loop fusion | flops 37748736 | bytes 58720256 | tf_op jit(solution)/shard_map/convert_element_type | solution.py:103
  (71 shorter events, 19.3 us)
Async XLA Ops:
  6.5 373.2 %all-reduce.2.cloned.1.call-start = ((), (), s32[]{:S(2)}) async-start(), calls=%async_computation | async-start | bytes 2097152 | tf_op jit(solution)/shard_map/psum | solution.py:92
  20.9 34.5 %copy-start = (s32[2]{0:T(128)S(1)}, s32[2]{0:T(128)}, u32[]{:S(2)}) copy-start(s32[2]{0:T(128)} %param.16) | copy-start | bytes 28
  20.9 37.1 %copy-start.2 = (s32[8]{0:T(128)S(1)}, s32[8]{0:T(128)}, u32[]{:S(2)}) copy-start(s32[8]{0:T(128)} %param.19) | copy-start | bytes 100
  20.9 16.3 %collective-permute-start = (bf16[128,32,128]{0,2,1:T(8,128)(2,1)S(1)}, bf16[128,32,128]{0,2,1:T(8,128)(2,1)S(1)}, u32[]{:S(2)}, u32[]{:S(2)}) collective-permute-start(bf16[128,32,128]{0,2,1:T(8,128)(2,1)S(1)} %get-tuple-element.10), channel_id=1, source_target_pairs={{0,32},{32,64},{64,96},{1,33},{33,65},{65,97},{2,34},{34,66},{66,9... | collective-permute-start | bytes 3145736 | tf_op jit(solution)/shard_map/ppermute | solution.py:21
  25.5 16.1 %collective-permute-start.1 = (bf16[128,32,128]{0,2,1:T(8,128)(2,1)S(1)}, bf16[128,32,128]{0,2,1:T(8,128)(2,1)S(1)}, u32[]{:S(2)}, u32[]{:S(2)}) collective-permute-start(bf16[128,32,128]{0,2,1:T(8,128)(2,1)S(1)} %get-tuple-element.12), channel_id=1, source_target_pairs={{32,0},{64,32},{96,64},{33,1},{65,33},{97,65},{34,2},{66,34},{98,6... | collective-permute-start | bytes 3145736 | tf_op jit(solution)/shard_map/ppermute | solution.py:23
  49.3 49.0 %collective-permute-start.2 = (bf16[128,320,32]{0,2,1:T(8,128)(2,1)}, bf16[128,320,32]{0,2,1:T(8,128)(2,1)}, u32[]{:S(2)}, u32[]{:S(2)}) collective-permute-start(bf16[128,320,32]{0,2,1:T(8,128)(2,1)} %get-tuple-element.6), channel_id=1, source_target_pairs={{0,1},{1,2},{2,3},{3,4},{4,5},{5,6},{6,7},{7,8},{8,9},{9,10},{10,1... | collective-permute-start | bytes 7864328 | tf_op jit(solution)/shard_map/ppermute | solution.py:21
  53.9 50.0 %collective-permute-start.3 = (bf16[128,320,32]{0,2,1:T(8,128)(2,1)}, bf16[128,320,32]{0,2,1:T(8,128)(2,1)}, u32[]{:S(2)}, u32[]{:S(2)}) collective-permute-start(bf16[128,320,32]{0,2,1:T(8,128)(2,1)} %get-tuple-element.8), channel_id=1, source_target_pairs={{1,0},{2,1},{3,2},{4,3},{5,4},{6,5},{7,6},{8,7},{9,8},{10,9},{11,1... | collective-permute-start | bytes 7864328 | tf_op jit(solution)/shard_map/ppermute | solution.py:23
  218.7 10.8 %copy-start.1 = (f32[2,128]{1,0:T(2,128)S(1)}, f32[2,128]{1,0:T(2,128)}, u32[]{:S(2)}) copy-start(f32[2,128]{1,0:T(2,128)} %param.17) | copy-start | bytes 3076
  435.2 31.4 %slice-start = ((s8[8388608]{0:T(1024)(128)(4,1)}), s8[4194304]{0:T(1024)(128)(4,1)S(1)}, s32[]{:S(2)}) async-start(s8[8388608]{0:T(1024)(128)(4,1)} %bitcast.128), calls=%async_computation.1 | async-start | bytes 8388608
  435.2 31.4 %slice-start.2 = ((s8[8388608]{0:T(1024)(128)(4,1)}), s8[4194304]{0:T(1024)(128)(4,1)S(1)}, s32[]{:S(2)}) async-start(s8[8388608]{0:T(1024)(128)(4,1)} %bitcast.130), calls=%async_computation.3 | async-start | bytes 8388608
  450.8 15.8 %slice-start.1 = ((s8[8388608]{0:T(1024)(128)(4,1)}), s8[4194304]{0:T(1024)(128)(4,1)S(1)}, s32[]{:S(2)}) async-start(s8[8388608]{0:T(1024)(128)(4,1)} %bitcast.128), calls=%async_computation.2 | async-start | bytes 8388608
  450.8 15.8 %slice-start.3 = ((s8[8388608]{0:T(1024)(128)(4,1)}), s8[4194304]{0:T(1024)(128)(4,1)S(1)}, s32[]{:S(2)}) async-start(s8[8388608]{0:T(1024)(128)(4,1)} %bitcast.130), calls=%async_computation.4 | async-start | bytes 8388608
Sparse Core Ops, SparseCore 0:
  228.3 151.4 all-reduce.1
where the time goes:
time: 510 us; the launch traced here: 505 us
  waiting for transfers between devices  210 us (41%)
  other arithmetic  123 us (24%)
  matrix products  76.2 us (15%)
  local copies, waits for them, and re-layouts  68 us (13%)
  between operations  15.9 us (3%)
  starting transfers between devices  12.6 us (2%)
    psum x1, waiting for transfers between devices, local(): totals = lax.psum(slotted, ('row', 'col'))  150 us
    ppermute x2, waiting for transfers between devices, extended_2(): lax.ppermute(tail, axis, [(i, (i + 1) % count) for i in range(ends)])  49.4 us
    convert_element_type x1, other arithmetic, local(): return cleaned.astype(jnp.bfloat16)  31.6 us
    concatenate x1, other arithmetic, extended_2(): jnp.concatenate([lax.ppermute(tail, axis, [(i, (i + 1) % count) for i in...  29 us
    another operation x12, other arithmetic, spd_solve(): factor = jnp.linalg.cholesky(matrix)  27.7 us
    concatenate x1, local copies, waits for them, and re-layouts, extended_2(): jnp.concatenate([lax.ppermute(tail, axis, [(i, (i + 1) % count) for i in...  26.4 us
    dot_general x1, matrix products, local(): jnp.einsum('cyx,xz->cyz', smooth, across_table, preferred_element_type=jn...  25.8 us
    another operation x8, other arithmetic, spd_solve(): lax.linalg.triangular_solve(factor, middle, left_side=True, lower=True, t...  23.6 us
  transfers between devices with their start and end apart: 5, of which 5 were waited for; matrix products, arithmetic and copies ran while one was open for 1% of the time, Pallas kernels for 0%

commit v1 on v0

v1 whole, which is shorter than its diff:
```python
import math
import functools
import jax
import jax.numpy as jnp
from jax import lax
from jax.experimental import pallas as pl
from jax.experimental.pallas import tpu as pltpu
from jax.sharding import PartitionSpec as P

HW = 32
MMAX = 8
TPR = 16
PLANE = 16
GROUP = 8
MESH = pl.DeviceIdType.MESH
HIGH = lax.Precision.HIGHEST


def gather_kernel(pk_ref, out_ref, first, slots, others, picked, last, s1, r1, s2, r2, s3, r3):
    row = lax.axis_index("row")
    col = lax.axis_index("col")
    part = lax.rem(col, PLANE)
    half = lax.div(col, PLANE)
    place = half * 4 + row

    def plane_peer(step):
        return (row, half * PLANE + lax.rem(part + step, PLANE))

    def group_peer(step):
        other = lax.rem(place + step, GROUP)
        return (lax.rem(other, 4), lax.div(other, 4) * PLANE + part)

    barrier = pltpu.get_barrier_semaphore()
    for step in range(1, PLANE):
        pl.semaphore_signal(barrier, inc=1, device_id=plane_peer(step), device_id_type=MESH)
    for step in range(1, GROUP):
        pl.semaphore_signal(barrier, inc=1, device_id=group_peer(step), device_id_type=MESH)
    pl.semaphore_wait(barrier, PLANE + GROUP - 2)

    one = []
    for step in range(1, PLANE):
        one.append(pltpu.make_async_remote_copy(
            src_ref=pk_ref.at[lax.rem(part + step, PLANE)], dst_ref=first.at[step],
            send_sem=s1.at[step], recv_sem=r1.at[step],
            device_id=plane_peer(step), device_id_type=MESH))
    for copy in one:
        copy.start()
    first[0] = pk_ref[part]
    for copy in one:
        copy.wait_recv()
    for region in range(8):
        total0 = jnp.zeros((8, 128), jnp.float32)
        total1 = jnp.zeros((8, 128), jnp.float32)
        for step in range(PLANE):
            flag = first[step, 2, region:region + 1, :]
            total0 = total0 + flag * first[step, 0]
            total1 = total1 + flag * first[step, 1]
        slots[region, 0] = total0
        slots[region, 1] = total1

    two = []
    for step in range(1, GROUP):
        two.append(pltpu.make_async_remote_copy(
            src_ref=slots, dst_ref=others.at[step],
            send_sem=s2.at[step], recv_sem=r2.at[step],
            device_id=group_peer(step), device_id_type=MESH))
    for copy in two:
        copy.start()
    for copy in two:
        copy.wait_recv()
    sums = []
    for region in range(8):
        pair = []
        for band in range(2):
            total = slots[region, band]
            for step in range(1, GROUP):
                total = total + others[step, region, band]
            pair.append(total)
        sums.append(pair)

    for step in range(PLANE):
        for band in range(2):
            total = jnp.zeros((8, 128), jnp.float32)
            for region in range(8):
                total = total + first[step, 2, region:region + 1, :] * sums[region][band]
            picked[step, band] = total
    three = []
    for step in range(1, PLANE):
        back = lax.rem(part + PLANE - step, PLANE)
        three.append(pltpu.make_async_remote_copy(
            src_ref=picked.at[step], dst_ref=last.at[part],
            send_sem=s3.at[step], recv_sem=r3.at[step],
            device_id=(row, half * PLANE + back), device_id_type=MESH))
    for copy in three:
        copy.start()
    last[part] = picked[0]
    for step in range(1, PLANE):
        ahead = lax.rem(part + step, PLANE)
        pltpu.make_async_remote_copy(
            src_ref=picked.at[step], dst_ref=last.at[ahead],
            send_sem=s3.at[step], recv_sem=r3.at[step],
            device_id=(row, half * PLANE + ahead), device_id_type=MESH).wait_recv()
    for index in range(PLANE):
        for band in range(2):
            out_ref[band, index * 8:index * 8 + 8, :] = last[index, band]
    for copy in one + two + three:
        copy.wait_send()


def region_grams(packed):
    return pl.pallas_call(
        gather_kernel,
        out_shape=jax.ShapeDtypeStruct((2, 128, 128), jnp.float32),
        in_specs=[pl.BlockSpec(memory_space=pltpu.VMEM)],
        out_specs=pl.BlockSpec(memory_space=pltpu.VMEM),
        scratch_shapes=[
            pltpu.VMEM((PLANE, 3, 8, 128), jnp.float32),
            pltpu.VMEM((8, 2, 8, 128), jnp.float32),
            pltpu.VMEM((GROUP, 8, 2, 8, 128), jnp.float32),
            pltpu.VMEM((PLANE, 2, 8, 128), jnp.float32),
            pltpu.VMEM((PLANE, 2, 8, 128), jnp.float32),
        ] + [pltpu.SemaphoreType.DMA((n,)) for n in (PLANE, PLANE, GROUP, GROUP, PLANE, PLANE)],
        compiler_params=pltpu.CompilerParams(collective_id=1, has_side_effects=True),
        name="region_sum",
    )(packed)


def weights_of(grams, priors, cheb_t, keep):
    lanes = lax.broadcasted_iota(jnp.int32, (8, 128), 1)
    subs = lax.broadcasted_iota(jnp.int32, (8, 128), 0)
    mats = []
    for band in range(2):
        blocks = []
        for i in range(16):
            block = grams[band][i * 8:i * 8 + 8, :]
            diag = jnp.where(lanes == subs + 8 * i, priors[band], 0.0)
            blocks.append(block / 524288.0 + diag)
        blocks.append(cheb_t)
        mats.append(blocks)
    for k in range(128):
        at, off = k // 8, k % 8
        hit = lanes[0:1, :] == k
        for band in range(2):
            m = mats[band]
            cols = [jnp.broadcast_to(b[:, k:k + 1], (8, 128)) for b in m]
            inv = 1.0 / cols[at][off:off + 1, :]
            line = m[at][off:off + 1, :] * inv
            line = jnp.where(hit, 1.0 - inv, line)
            mats[band] = [b - c * line for b, c in zip(m, cols)]
    out = []
    for band in range(2):
        mixed = mats[band][16] * keep
        kept = cheb_t * keep
        small = lax.dot_general(kept, mixed, (((1,), (1,)), ((), ())), precision=HIGH,
                                preferred_element_type=jnp.float32)
        eye = (lax.broadcasted_iota(jnp.int32, (8, 8), 0) == lax.broadcasted_iota(jnp.int32, (8, 8), 1))
        small = small + jnp.where(eye, 1.0 - keep[:, 0:8], 0.0)
        out.append((small, mixed))
    weights = []
    for small, mixed in out:
        for k in range(8):
            fac = small[:, k:k + 1]
            inv = 1.0 / fac[k:k + 1, :]
            shift = jnp.where(subs[:, 0:1] == k, 1.0, 0.0)
            fac = fac - shift
            srow = small[k:k + 1, :] * inv
            mrow = mixed[k:k + 1, :] * inv
            small = small - fac * srow
            mixed = mixed - fac * mrow
        weights.append(mixed)
    return weights


def solve_kernel(gram_ref, prior_ref, cheb_ref, keep_ref, out_ref):
    cheb_t = cheb_ref[...]
    keep = keep_ref[...]
    grams = [gram_ref[0], gram_ref[1]]
    priors = [prior_ref[0:1, :], prior_ref[1:2, :]]
    weights = weights_of(grams, priors, cheb_t, keep)
    kept = cheb_t * keep
    for band in range(2):
        proj = lax.dot_general(kept, weights[band], (((0,), (0,)), ((), ())), precision=HIGH,
                               preferred_element_type=jnp.float32)
        out_ref[band] = proj.astype(jnp.bfloat16)


def projectors(grams, prior_var, cheb_t, keep):
    return pl.pallas_call(
        solve_kernel,
        out_shape=jax.ShapeDtypeStruct((2, 128, 128), jnp.bfloat16),
        in_specs=[pl.BlockSpec(memory_space=pltpu.VMEM)] * 4,
        out_specs=pl.BlockSpec(memory_space=pltpu.VMEM),
        name="solve",
    )(grams, prior_var, cheb_t, keep)


def extended_2(cells, sides, width):
    for axis, dim in sides:
        count = lax.axis_size(axis)
        ends = count - 1
        head = lax.slice_in_dim(cells, 0, width, axis=dim)
        tail = lax.slice_in_dim(cells, cells.shape[dim] - width, cells.shape[dim], axis=dim)
        cells = jnp.concatenate(
            [
                lax.ppermute(tail, axis, [(i, (i + 1) % count) for i in range(ends)]),
                cells,
                lax.ppermute(head, axis, [((i + 1) % count, i) for i in range(ends)]),
            ],
            axis=dim,
        )
    return cells


def raised(offsets, half_width):
    spread = half_width.astype(jnp.float32)
    inside = jnp.abs(offsets) <= spread
    values = (1.0 + jnp.cos(math.pi * offsets / (spread + 1.0))) / (2.0 * spread + 2.0)
    return jnp.where(inside, values, jnp.zeros_like(values))


def toeplitz(length, half_width):
    inputs = jnp.arange(length + 2 * HW, dtype=jnp.float32)[:, None]
    outputs = jnp.arange(length, dtype=jnp.float32)[None, :]
    offsets = inputs - outputs - HW
    return raised(offsets, half_width).astype(jnp.bfloat16)


def chebyshev(chan_count, degree):
    position = (2.0 * jnp.arange(chan_count, dtype=jnp.float32) + 1.0) / chan_count - 1.0
    terms = [jnp.ones_like(position), position]
    for order in range(2, degree):
        terms.append(2.0 * position * terms[-1] - terms[-2])
    return jnp.stack(terms[:degree], axis=0)


def local(sky, kernel_widths, prior_var, tile_region, region_rank):
    chan_count, tile_rows, tile_cols = sky.shape
    down_table = toeplitz(tile_rows, kernel_widths[0])
    across_table = toeplitz(tile_cols, kernel_widths[1])
    extended = extended_2(sky, (("row", 1), ("col", 2)), HW)
    smooth = jnp.einsum(
        "cyx,yz->czx", extended, down_table, preferred_element_type=jnp.float32
    ).astype(jnp.bfloat16)
    coarse = jnp.einsum(
        "cyx,xz->cyz", smooth, across_table, preferred_element_type=jnp.float32
    ).astype(jnp.bfloat16)
    fine = (sky.astype(jnp.float32) - coarse.astype(jnp.float32)).astype(jnp.bfloat16)
    coarse_gram = jnp.einsum("cyx,dyx->cd", coarse, coarse, preferred_element_type=jnp.float32)
    fine_gram = jnp.einsum("cyx,dyx->cd", fine, fine, preferred_element_type=jnp.float32)
    region = tile_region[0, 0]
    flags = jnp.broadcast_to((jnp.arange(8) == region).astype(jnp.float32)[None, :, None], (PLANE, 8, 128))
    packed = jnp.stack(
        [coarse_gram.reshape(PLANE, 8, 128), fine_gram.reshape(PLANE, 8, 128), flags], axis=1)
    own_gram = region_grams(packed)
    keep_rank = lax.dynamic_index_in_dim(region_rank, region, 0, keepdims=False)
    keep = jnp.broadcast_to((jnp.arange(8) < keep_rank).astype(jnp.float32)[:, None], (8, 128))
    proj = projectors(own_gram, prior_var, chebyshev(chan_count, MMAX), keep)
    removed = jnp.einsum("ij,jyx->iyx", proj[0], coarse, preferred_element_type=jnp.float32)
    removed = removed + jnp.einsum("ij,jyx->iyx", proj[1], fine, preferred_element_type=jnp.float32)
    cleaned = coarse.astype(jnp.float32) + fine.astype(jnp.float32) - removed
    return cleaned.astype(jnp.bfloat16)


def solution(mesh):
    return jax.shard_map(
        local,
        mesh=mesh,
        in_specs=(P(None, "row", "col"), P(), P(), P("row", "col"), P()),
        out_specs=P(None, "row", "col"),
        check_vma=False,
    )
```

time: 510 us -> 332 us (0.65)
  waiting for transfers between devices: 210 us -> 58.1 us
  other arithmetic: 123 us -> 69.9 us
  Pallas kernels: 0 us -> 41.7 us
  between operations: 15.9 us -> 2.3 us
    psum x1 -> x0, waiting for transfers between devices: 150 us -> none  [local(): totals = lax.psum(slotted, ('row', 'col'))]
    another operation x21 -> x1, other arithmetic: 51.3 us -> 0.68 us  [local(): jnp.stack([coarse_gram.reshape(PLANE, 8, 128), fine_gram.reshape(PLANE, 8...]
    pallas_call x0 -> x2, Pallas kernels: none -> 41.7 us  [the longest x1 28.2 us: region_grams(): pl.pallas_call(gather_kernel, out_shape=jax.ShapeDtypeStruct((2, 128, 128...]
    dot_general x6 -> x2, matrix products: 32.6 us -> 31.6 us  [the longest x1 16 us: local(): jnp.einsum('ij,jyx->iyx', proj[1], fine, preferred_element_type=jnp.float32)]
  transfers between devices with their start and end apart: 5 -> 4, of which waited for: 5 -> 4; matrix products, arithmetic and copies ran while one was open for 1% -> 1% of each run, Pallas kernels for 0% -> 0%
where the time goes in v1:
time: 332 us; the launch traced here: 327 us
  matrix products  73.6 us (22%)
  other arithmetic  69.9 us (21%)
  local copies, waits for them, and re-layouts  68.5 us (21%)
  waiting for transfers between devices  58.1 us (18%)
  Pallas kernels  41.7 us (13%)
  starting transfers between devices  12.6 us (4%)
    ppermute x2, waiting for transfers between devices, extended_2(): lax.ppermute(tail, axis, [(i, (i + 1) % count) for i in range(ends)])  48.1 us
    convert_element_type x1, other arithmetic, local(): return cleaned.astype(jnp.bfloat16)  31.7 us
    concatenate x1, other arithmetic, extended_2(): jnp.concatenate([lax.ppermute(tail, axis, [(i, (i + 1) % count) for i in...  29 us
    pallas_call x1, Pallas kernels, region_grams(): pl.pallas_call(gather_kernel, out_shape=jax.ShapeDtypeStruct((2, 128, 128...  28.2 us
    concatenate x1, local copies, waits for them, and re-layouts, extended_2(): jnp.concatenate([lax.ppermute(tail, axis, [(i, (i + 1) % count) for i in...  26.2 us
    dot_general x1, matrix products, local(): jnp.einsum('cyx,xz->cyz', smooth, across_table, preferred_element_type=jn...  25.8 us
    dot_general x1, matrix products, local(): jnp.einsum('ij,jyx->iyx', proj[1], fine, preferred_element_type=jnp.float32)  16 us
    dot_general x1, matrix products, local(): jnp.einsum('ij,jyx->iyx', proj[0], coarse, preferred_element_type=jnp.flo...  15.6 us
  transfers between devices with their start and end apart: 4, of which 4 were waited for; matrix products, arithmetic and copies ran while one was open for 1% of the time, Pallas kernels for 0%

profile of v1, /device:TPU:1, one launch (start us, length us, event | category | flops | bytes accessed | tf_op | source)
XLA Modules:
  0.0 326.7 jit_solution(5127065595382907569)
XLA Ops:
  0.0 12.7 %copy.14 = bf16[128,256,128]{0,2,1:T(8,128)(2,1)} copy(bf16[128,256,128]{2,1,0:T(8,128)(2,1)} %param.5) | data formatting | bytes 16777216 | tf_op args[0]
  12.7 1.7 fusion.49
  14.4 4.6 %collective-permute-start = (bf16[128,32,128]{0,2,1:T(8,128)(2,1)S(1)}, bf16[128,32,128]{0,2,1:T(8,128)(2,1)S(1)}, u32[]{:S(2)}, u32[]{:S(2)}) collective-permute-start(bf16[128,32,128]{0,2,1:T(8,128)(2,1)S(1)} %get-tuple-element.7), channel_id=1, source_target_pairs={{0,32},{32,64},{64,96},{1,33},{33,65},{65,97},{2,34},{34,66},{66,9... | collective-permute-start | bytes 3145736 | tf_op jit(solution)/shard_map/ppermute | solution.py:205
  19.0 1.9 collective-permute-start.1
  20.9 9.8 %collective-permute-done = bf16[128,32,128]{0,2,1:T(8,128)(2,1)S(1)} collective-permute-done((bf16[128,32,128]{0,2,1:T(8,128)(2,1)S(1)}, bf16[128,32,128]{0,2,1:T(8,128)(2,1)S(1)}, u32[]{:S(2)}, u32[]{:S(2)}) %collective-permute-start) | collective-permute-done | bytes 1048608 | tf_op jit(solution)/shard_map/ppermute | solution.py:205
  30.7 4.4 %collective-permute-done.1 = bf16[128,32,128]{0,2,1:T(8,128)(2,1)S(1)} collective-permute-done((bf16[128,32,128]{0,2,1:T(8,128)(2,1)S(1)}, bf16[128,32,128]{0,2,1:T(8,128)(2,1)S(1)}, u32[]{:S(2)}, u32[]{:S(2)}) %collective-permute-start.1) | collective-permute-done | bytes 1048608 | tf_op jit(solution)/shard_map/ppermute | solution.py:207
  35.1 7.7 %pad_maximum_fusion.3 = (bf16[128,320,32]{0,2,1:T(8,128)(2,1)}, bf16[128,320,32]{0,2,1:T(8,128)(2,1)}) fusion(bf16[128,32,128]{0,2,1:T(8,128)(2,1)S(1)} %collective-permute-done.1, bf16[128,256,128]{0,2,1:T(8,128)(2,1)} %copy.14, bf16[128,32,128]{0,2,1:T(8,128)(2,1)S(1)} %collective-permute-done), kind=kLoop, calls=%fused_computation.18 | loop fusion | flops 15728640 | bytes 15728640 | tf_op jit(solution)/shard_map/slice | solution.py:202
  42.8 4.6 %collective-permute-start.2 = (bf16[128,320,32]{0,2,1:T(8,128)(2,1)}, bf16[128,320,32]{0,2,1:T(8,128)(2,1)}, u32[]{:S(2)}, u32[]{:S(2)}) collective-permute-start(bf16[128,320,32]{0,2,1:T(8,128)(2,1)} %get-tuple-element.5), channel_id=1, source_target_pairs={{0,1},{1,2},{2,3},{3,4},{4,5},{5,6},{6,7},{7,8},{8,9},{9,10},{10,1... | collective-permute-start | bytes 7864328 | tf_op jit(solution)/shard_map/ppermute | solution.py:205
  47.4 1.5 collective-permute-start.3
  53.5 38.3 %collective-permute-done.2 = bf16[128,320,32]{0,2,1:T(8,128)(2,1)} collective-permute-done((bf16[128,320,32]{0,2,1:T(8,128)(2,1)}, bf16[128,320,32]{0,2,1:T(8,128)(2,1)}, u32[]{:S(2)}, u32[]{:S(2)}) %collective-permute-start.2) | collective-permute-done | bytes 2621472 | tf_op jit(solution)/shard_map/ppermute | solution.py:205
  91.8 5.6 %collective-permute-done.3 = bf16[128,320,32]{0,2,1:T(8,128)(2,1)} collective-permute-done((bf16[128,320,32]{0,2,1:T(8,128)(2,1)}, bf16[128,320,32]{0,2,1:T(8,128)(2,1)}, u32[]{:S(2)}, u32[]{:S(2)}) %collective-permute-start.3) | collective-permute-done | bytes 2621472 | tf_op jit(solution)/shard_map/ppermute | solution.py:207
  97.4 29.0 %pad_maximum_fusion = bf16[128,320,192]{0,2,1:T(8,128)(2,1)} fusion(bf16[128,320,32]{0,2,1:T(8,128)(2,1)} %collective-permute-done.3, bf16[128,32,128]{0,2,1:T(8,128)(2,1)S(1)} %collective-permute-done.1, bf16[128,256,128]{0,2,1:T(8,128)(2,1)} %copy.14, bf16[128,32,128]{0,2,1:T(8,128)(2,1)S(1)} %collective-permute-done, ...), kind=kLoop, calls=%fused_computation.6 | loop fusion | flops 78643200 | bytes 31457280 | tf_op jit(solution)/shard_map/concatenate | solution.py:203
  126.5 26.2 %copy.25 = bf16[128,320,192]{1,2,0:T(8,128)(2,1)} copy(bf16[128,320,192]{0,2,1:T(8,128)(2,1)} %pad_maximum_fusion) | data formatting | bytes 31457280 | tf_op jit(solution)/shard_map/concatenate | solution.py:203
  152.7 25.8 %fusion = (bf16[128,256,128]{2,1,0:T(8,128)(2,1)}, bf16[128,256,128]{2,1,0:T(8,128)(2,1)}) fusion(bf16[128,256,128]{2,1,0:T(8,128)(2,1)} %param.5, f32[]{:T(128)S(6)} %add.149, f32[]{:T(128)S(6)} %add.146, f32[]{:T(128)} %bitcast.4, bf16[128,320,192]{1,2,0:T(8,128)(2,1)} %copy.25, f32[]{:T(128)S(6)} %add.145, f32[]{:T(128)S(6)} %add.142, f32[]{:T(128)} %bitcast.1), kind=kOutput, calls=%fused_computation.2 | convolution fusion | flops 5665472512 | bytes 40894488 | tf_op jit(solution)/shard_map/cyx,xz->cyz/dot_general | solution.py:244
  178.5 12.6 %copy.19 = bf16[128,256,128]{1,0,2:T(8,128)(2,1)} copy(bf16[128,256,128]{2,1,0:T(8,128)(2,1)} %get-tuple-element.11) | data formatting | bytes 16777216 | tf_op jit(solution)/shard_map/convert_element_type | solution.py:247
  191.0 8.1 %convolution_bitcast_fusion = f32[16,1,8,128]{3,2,1,0:T(8,128)S(1)} fusion(bf16[128,256,128]{1,0,2:T(8,128)(2,1)} %copy.19), kind=kOutput, calls=%fused_computation.19 | convolution fusion | flops 1073741824 | bytes 8454144 | tf_op jit(solution)/shard_map/cyx,dyx->cd/dot_general | solution.py:249
  199.1 12.8 %copy.17 = bf16[128,256,128]{1,0,2:T(8,128)(2,1)} copy(bf16[128,256,128]{2,1,0:T(8,128)(2,1)} %get-tuple-element.12) | data formatting | bytes 16777216 | tf_op jit(solution)/shard_map/convert_element_type | solution.py:246
  211.9 8.1 %convolution_bitcast_fusion.1 = f32[16,1,8,128]{3,2,1,0:T(8,128)S(1)} fusion(bf16[128,256,128]{1,0,2:T(8,128)(2,1)} %copy.17), kind=kOutput, calls=%fused_computation.20 | convolution fusion | flops 1073741824 | bytes 8454144 | tf_op jit(solution)/shard_map/cyx,dyx->cd/dot_general | solution.py:248
  220.1 0.7 pad_maximum_fusion.4.pk_ref
  220.7 28.2 %region_sum.1.gram_ref = f32[2,128,128]{2,1,0:T(8,128)} custom-call(f32[16,3,8,128]{3,2,1,0:T(8,128)} %pad_maximum_fusion.4.pk_ref), custom_call_target="tpu_custom_call" | custom-call | tf_op jit(solution)/shard_map/region_sum/pallas_call | solution.py:111
  249.6 13.5 %solve.1 = bf16[2,128,128]{2,1,0:T(8,128)(2,1)} custom-call(f32[2,128,128]{2,1,0:T(8,128)} %region_sum.1.gram_ref, f32[2,128]{1,0:T(2,128)} %prior_ref.1, f32[8,128]{1,0:T(8,128)} %stack.5.cheb_ref, f32[8,128]{1,0:T(8,128)} %broadcast_in_dim.8.keep_ref), custom_call_target="tpu_custom_call" | custom-call | tf_op jit(solution)/shard_map/solve/pallas_call | solution.py:188
  263.1 16.0 %fusion.8 = f32[128,256,128]{2,0,1:T(8,128)} fusion(bf16[128,256,128]{2,1,0:T(8,128)(2,1)} %get-tuple-element.11, bf16[2,128,128]{2,1,0:T(8,128)(2,1)} %solve.1), kind=kOutput, calls=%fused_computation.11 | convolution fusion | flops 1073741824 | bytes 25198592 | tf_op jit(solution)/shard_map/ij,jyx->iyx/dot_general | solution.py:259
  279.1 15.6 %fusion.10 = f32[128,256,128]{2,0,1:T(8,128)} fusion(bf16[128,256,128]{2,1,0:T(8,128)(2,1)} %get-tuple-element.12, bf16[2,128,128]{2,1,0:T(8,128)(2,1)S(1)} %copy-done), kind=kOutput, calls=%fused_computation.13 | convolution fusion | flops 1073741824 | bytes 25198592 | tf_op jit(solution)/shard_map/ij,jyx->iyx/dot_general | solution.py:258
  294.8 31.7 %fusion.2 = bf16[128,256,128]{2,1,0:T(8,128)(2,1)} fusion(bf16[128,256,128]{2,1,0:T(8,128)(2,1)S(1)} %bitcast.49, f32[128,256,128]{2,0,1:T(8,128)} %fusion.8, f32[128,256,128]{2,0,1:T(8,128)} %fusion.10, bf16[128,256,128]{2,1,0:T(8,128)(2,1)S(1)} %bitcast.51), kind=kLoop, calls=%fused_computation.4 | loop fusion | flops 37748736 | bytes 58720256 | tf_op jit(solution)/shard_map/convert_element_type | solution.py:261
  (28 shorter events, 3.4 us)
Async XLA Ops:
  14.3 34.6 %copy-start.1 = (s32[2]{0:T(128)S(1)}, s32[2]{0:T(128)}, u32[]{:S(2)}) copy-start(s32[2]{0:T(128)} %param.6) | copy-start | bytes 28
  14.3 37.2 %copy-start.2 = (s32[8]{0:T(128)S(1)}, s32[8]{0:T(128)}, u32[]{:S(2)}) copy-start(s32[8]{0:T(128)} %param.9) | copy-start | bytes 100
  14.4 16.3 %collective-permute-start = (bf16[128,32,128]{0,2,1:T(8,128)(2,1)S(1)}, bf16[128,32,128]{0,2,1:T(8,128)(2,1)S(1)}, u32[]{:S(2)}, u32[]{:S(2)}) collective-permute-start(bf16[128,32,128]{0,2,1:T(8,128)(2,1)S(1)} %get-tuple-element.7), channel_id=1, source_target_pairs={{0,32},{32,64},{64,96},{1,33},{33,65},{65,97},{2,34},{34,66},{66,9... | collective-permute-start | bytes 3145736 | tf_op jit(solution)/shard_map/ppermute | solution.py:205
  19.0 16.1 %collective-permute-start.1 = (bf16[128,32,128]{0,2,1:T(8,128)(2,1)S(1)}, bf16[128,32,128]{0,2,1:T(8,128)(2,1)S(1)}, u32[]{:S(2)}, u32[]{:S(2)}) collective-permute-start(bf16[128,32,128]{0,2,1:T(8,128)(2,1)S(1)} %get-tuple-element.8), channel_id=1, source_target_pairs={{32,0},{64,32},{96,64},{33,1},{65,33},{97,65},{34,2},{66,34},{98,6... | collective-permute-start | bytes 3145736 | tf_op jit(solution)/shard_map/ppermute | solution.py:207
  42.8 49.0 %collective-permute-start.2 = (bf16[128,320,32]{0,2,1:T(8,128)(2,1)}, bf16[128,320,32]{0,2,1:T(8,128)(2,1)}, u32[]{:S(2)}, u32[]{:S(2)}) collective-permute-start(bf16[128,320,32]{0,2,1:T(8,128)(2,1)} %get-tuple-element.5), channel_id=1, source_target_pairs={{0,1},{1,2},{2,3},{3,4},{4,5},{5,6},{6,7},{7,8},{8,9},{9,10},{10,1... | collective-permute-start | bytes 7864328 | tf_op jit(solution)/shard_map/ppermute | solution.py:205
  47.4 50.0 %collective-permute-start.3 = (bf16[128,320,32]{0,2,1:T(8,128)(2,1)}, bf16[128,320,32]{0,2,1:T(8,128)(2,1)}, u32[]{:S(2)}, u32[]{:S(2)}) collective-permute-start(bf16[128,320,32]{0,2,1:T(8,128)(2,1)} %get-tuple-element.6), channel_id=1, source_target_pairs={{1,0},{2,1},{3,2},{4,3},{5,4},{6,5},{7,6},{8,7},{9,8},{10,9},{11,1... | collective-permute-start | bytes 7864328 | tf_op jit(solution)/shard_map/ppermute | solution.py:207
  263.1 16.0 %copy-start = (bf16[2,128,128]{2,1,0:T(8,128)(2,1)S(1)}, bf16[2,128,128]{2,1,0:T(8,128)(2,1)}, u32[]{:S(2)}) copy-start(bf16[2,128,128]{2,1,0:T(8,128)(2,1)} %solve.1) | copy-start | bytes 196612
  263.1 31.6 %slice-start = ((s8[8388608]{0:T(1024)(128)(4,1)}), s8[4194304]{0:T(1024)(128)(4,1)S(1)}, s32[]{:S(2)}) async-start(s8[8388608]{0:T(1024)(128)(4,1)} %bitcast.48), calls=%async_computation | async-start | bytes 8388608
  263.1 31.6 %slice-start.2 = ((s8[8388608]{0:T(1024)(128)(4,1)}), s8[4194304]{0:T(1024)(128)(4,1)S(1)}, s32[]{:S(2)}) async-start(s8[8388608]{0:T(1024)(128)(4,1)} %bitcast.50), calls=%async_computation.2 | async-start | bytes 8388608
  279.1 15.6 %slice-start.1 = ((s8[8388608]{0:T(1024)(128)(4,1)}), s8[4194304]{0:T(1024)(128)(4,1)S(1)}, s32[]{:S(2)}) async-start(s8[8388608]{0:T(1024)(128)(4,1)} %bitcast.48), calls=%async_computation.1 | async-start | bytes 8388608
  279.1 15.6 %slice-start.3 = ((s8[8388608]{0:T(1024)(128)(4,1)}), s8[4194304]{0:T(1024)(128)(4,1)S(1)}, s32[]{:S(2)}) async-start(s8[8388608]{0:T(1024)(128)(4,1)} %bitcast.50), calls=%async_computation.3 | async-start | bytes 8388608

commit v2 on v1

v2 whole, which is shorter than its diff:
```python
import math
import jax
import jax.numpy as jnp
from jax import lax
from jax.experimental import pallas as pl
from jax.experimental.pallas import tpu as pltpu
from jax.sharding import PartitionSpec as P

HW = 32
MMAX = 8
TPR = 16
PLANE = 16
GROUP = 8
CHANS = 128
CHUNK = 64
ORDER = (1, 2, 0, 3)
MESH = pl.DeviceIdType.MESH
HIGH = lax.Precision.HIGHEST
NT = (((1,), (1,)), ((), ()))


def front_kernel(sky_ref, table_ref, flag_ref, bands_ref, gram_ref,
                 skyx, smooth, out_l, out_r, in_l, in_r, across, pick, flat_c, flat_f, stage, grams, pieces,
                 first, slots, others, picked, last,
                 sky_sem, ys, yr, xs, xr, stage_sem, s1, r1, s2, r2, s3, r3):
    row = lax.axis_index("row")
    col = lax.axis_index("col")
    part = lax.rem(col, PLANE)
    half = lax.div(col, PLANE)
    place = half * 4 + row

    def plane_peer(step):
        return (row, half * PLANE + lax.rem(part + step, PLANE))

    def group_peer(step):
        other = lax.rem(place + step, GROUP)
        return (lax.rem(other, 4), lax.div(other, 4) * PLANE + part)

    barrier = pltpu.get_barrier_semaphore()
    for step in (1, 31):
        pl.semaphore_signal(barrier, inc=1, device_id=(row, lax.rem(col + step, 32)), device_id_type=MESH)
    for step in range(1, GROUP):
        pl.semaphore_signal(barrier, inc=1, device_id=group_peer(step), device_id_type=MESH)
    for step in range(1, PLANE):
        pl.semaphore_signal(barrier, inc=1, device_id=plane_peer(step), device_id_type=MESH)

    load = pltpu.make_async_copy(sky_ref, skyx.at[:, HW:HW + 256, :], sky_sem)
    load.start()

    zero = jnp.zeros((512, 256), jnp.bfloat16)
    own = table_ref[HW:HW + 128, :]
    for h in range(2):
        across[h] = zero
        across[h, 0:128, 0:128] = own
        across[h, 128:256, 128:256] = own
        for k in range(2):
            base = HW * (2 * h + k)
            across[h, 256 + base:256 + base + HW, 128 * k:128 * k + 128] = table_ref[0:HW, :]
            across[h, 384 + base:384 + base + HW, 128 * k:128 * k + 128] = table_ref[160:192, :]
    source = lax.broadcasted_iota(jnp.int32, (512, 256), 0)
    target = lax.broadcasted_iota(jnp.int32, (512, 256), 1)
    lane = target % 128
    wanted = (lane // HW) * 128 + lane % HW + jnp.where(target >= 128, 96, 0)
    pick[...] = jnp.where(source == wanted, 1.0, 0.0).astype(jnp.bfloat16)
    down = table_ref[192:256, :]
    grams[...] = jnp.zeros((2, 128, 128), jnp.float32)

    @pl.when(row == 0)
    def _():
        skyx[:, 0:HW, :] = jnp.zeros((CHANS, HW, 128), jnp.bfloat16)

    @pl.when(row == 3)
    def _():
        skyx[:, HW + 256:, :] = jnp.zeros((CHANS, HW, 128), jnp.bfloat16)

    @pl.when(col == 0)
    def _():
        in_l[...] = jnp.zeros(in_l.shape, jnp.bfloat16)

    @pl.when(col == 31)
    def _():
        in_r[...] = jnp.zeros(in_r.shape, jnp.bfloat16)

    pl.semaphore_wait(barrier, PLANE + GROUP)

    to_next = pltpu.make_async_remote_copy(
        src_ref=sky_ref.at[:, 256 - HW:256, :], dst_ref=skyx.at[:, 0:HW, :],
        send_sem=ys.at[0], recv_sem=yr.at[0], device_id=(lax.rem(row + 1, 4), col), device_id_type=MESH)
    to_last = pltpu.make_async_remote_copy(
        src_ref=sky_ref.at[:, 0:HW, :], dst_ref=skyx.at[:, HW + 256:, :],
        send_sem=ys.at[1], recv_sem=yr.at[1], device_id=(lax.rem(row + 3, 4), col), device_id_type=MESH)

    @pl.when(row < 3)
    def _():
        to_next.start()

    @pl.when(row > 0)
    def _():
        to_last.start()

    load.wait()

    def to_right(j):
        return pltpu.make_async_remote_copy(
            src_ref=out_r.at[j], dst_ref=in_l.at[j], send_sem=xs.at[0, j], recv_sem=xr.at[0, j],
            device_id=(row, lax.rem(col + 1, 32)), device_id_type=MESH)

    def to_left(j):
        return pltpu.make_async_remote_copy(
            src_ref=out_l.at[j], dst_ref=in_r.at[j], send_sem=xs.at[1, j], recv_sem=xr.at[1, j],
            device_id=(row, lax.rem(col + 31, 32)), device_id_type=MESH)

    for j in ORDER:
        if j == 0:
            @pl.when(row > 0)
            def _():
                to_next.wait_recv()
        if j == 3:
            @pl.when(row < 3)
            def _():
                to_last.wait_recv()

        def smooth_some(step, carry, j=j):
            c0 = step * 16
            for p in range(8):
                c = c0 + 2 * p
                window = jnp.concatenate(
                    [skyx[c, CHUNK * j:CHUNK * j + 128, :], skyx[c + 1, CHUNK * j:CHUNK * j + 128, :]], axis=1)
                result = jnp.dot(down, window, preferred_element_type=jnp.float32).astype(jnp.bfloat16)
                smooth[j, c] = result[:, 0:128]
                smooth[j, c + 1] = result[:, 128:256]
            return carry

        lax.fori_loop(0, 8, smooth_some, 0)

        def pack_some(step, carry, j=j):
            c0 = step * 32
            wide = jnp.concatenate(
                [smooth[j, pl.ds(c0, 32), 16 * q:16 * q + 16, :].reshape(512, 128) for q in range(4)], axis=1)
            edges = jnp.dot(wide, pick[...], preferred_element_type=jnp.float32).astype(jnp.bfloat16)
            out_l[j, pl.ds(c0, 32)] = edges[:, 0:128].reshape(32, 16, 128)
            out_r[j, pl.ds(c0, 32)] = edges[:, 128:256].reshape(32, 16, 128)
            return carry

        lax.fori_loop(0, 4, pack_some, 0)

        @pl.when(col < 31)
        def _(j=j):
            to_right(j).start()

        @pl.when(col > 0)
        def _(j=j):
            to_left(j).start()

    def put(h, base):
        return pltpu.make_async_copy(stage.at[h], bands_ref.at[pl.ds(base, 32)], stage_sem.at[h])

    for turn, j in enumerate(ORDER):
        @pl.when(col > 0)
        def _(j=j):
            to_right(j).wait_recv()

        @pl.when(col < 31)
        def _(j=j):
            to_left(j).wait_recv()

        for h in range(2):
            def coarse_some(step, carry, j=j, h=h):
                c0 = step * 32
                wide = jnp.concatenate(
                    [smooth[j, pl.ds(c0, 32), 32 * h + 16 * k:32 * h + 16 * k + 16, :].reshape(512, 128)
                     for k in range(2)]
                    + [in_l[j, pl.ds(c0, 32)].reshape(512, 128), in_r[j, pl.ds(c0, 32)].reshape(512, 128)], axis=1)
                both = jnp.dot(wide, across[h], preferred_element_type=jnp.float32)
                both = both.astype(jnp.bfloat16).astype(jnp.float32)
                for k in range(2):
                    begin = HW + CHUNK * j + 32 * h + 16 * k
                    value = both[:, 128 * k:128 * k + 128]
                    pixels = skyx[pl.ds(c0, 32), begin:begin + 16, :].reshape(512, 128).astype(jnp.float32)
                    flat_c[pl.ds(2048 * k + c0 * 16, 512), :] = value
                    flat_f[pl.ds(2048 * k + c0 * 16, 512), :] = pixels - value
                return carry

            lax.fori_loop(0, 4, coarse_some, 0)
            if turn > 0:
                put(h, 0).wait()

            def turn_some(k, carry, h=h):
                for y0 in range(0, 16, 4):
                    for band, flat in ((0, flat_c), (1, flat_f)):
                        lines = []
                        for y in range(y0, y0 + 4):
                            line = flat[pl.ds(2048 * k + y, 128, stride=16), :].astype(jnp.bfloat16)
                            stage[h, 16 * k + y, 128 * band:128 * band + 128, :] = line
                            lines.append(line)
                        wide = jnp.concatenate(lines, axis=1)
                        grams[band] = grams[band] + lax.dot_general(
                            wide, wide, NT, preferred_element_type=jnp.float32)
                return carry

            lax.fori_loop(0, 2, turn_some, 0)
            put(h, CHUNK * j + 32 * h).start()

    for q in range(PLANE):
        pieces[q, 0] = grams[0, 8 * q:8 * q + 8, :]
        pieces[q, 1] = grams[1, 8 * q:8 * q + 8, :]
        pieces[q, 2] = flag_ref[...]
    one = []
    for step in range(1, PLANE):
        one.append(pltpu.make_async_remote_copy(
            src_ref=pieces.at[lax.rem(part + step, PLANE)], dst_ref=first.at[step],
            send_sem=s1.at[step], recv_sem=r1.at[step],
            device_id=plane_peer(step), device_id_type=MESH))
    for copy in one:
        copy.start()
    first[0] = pieces[part]
    for copy in one:
        copy.wait_recv()
    for region in range(8):
        total0 = jnp.zeros((8, 128), jnp.float32)
        total1 = jnp.zeros((8, 128), jnp.float32)
        for step in range(PLANE):
            flag = first[step, 2, region:region + 1, :]
            total0 = total0 + flag * first[step, 0]
            total1 = total1 + flag * first[step, 1]
        slots[region, 0] = total0
        slots[region, 1] = total1

    two = []
    for step in range(1, GROUP):
        two.append(pltpu.make_async_remote_copy(
            src_ref=slots, dst_ref=others.at[step],
            send_sem=s2.at[step], recv_sem=r2.at[step],
            device_id=group_peer(step), device_id_type=MESH))
    for copy in two:
        copy.start()
    for copy in two:
        copy.wait_recv()
    sums = []
    for region in range(8):
        pair = []
        for band in range(2):
            total = slots[region, band]
            for step in range(1, GROUP):
                total = total + others[step, region, band]
            pair.append(total)
        sums.append(pair)

    for step in range(PLANE):
        for band in range(2):
            total = jnp.zeros((8, 128), jnp.float32)
            for region in range(8):
                total = total + first[step, 2, region:region + 1, :] * sums[region][band]
            picked[step, band] = total
    three = []
    for step in range(1, PLANE):
        back = lax.rem(part + PLANE - step, PLANE)
        three.append(pltpu.make_async_remote_copy(
            src_ref=picked.at[step], dst_ref=last.at[part],
            send_sem=s3.at[step], recv_sem=r3.at[step],
            device_id=(row, half * PLANE + back), device_id_type=MESH))
    for copy in three:
        copy.start()
    last[part] = picked[0]
    for step in range(1, PLANE):
        ahead = lax.rem(part + step, PLANE)
        pltpu.make_async_remote_copy(
            src_ref=picked.at[step], dst_ref=last.at[ahead],
            send_sem=s3.at[step], recv_sem=r3.at[step],
            device_id=(row, half * PLANE + ahead), device_id_type=MESH).wait_recv()
    for index in range(PLANE):
        for band in range(2):
            gram_ref[band, index * 8:index * 8 + 8, :] = last[index, band]

    for h in range(2):
        put(h, 0).wait()

    @pl.when(row < 3)
    def _():
        to_next.wait_send()

    @pl.when(row > 0)
    def _():
        to_last.wait_send()

    @pl.when(col < 31)
    def _():
        for j in ORDER:
            to_right(j).wait_send()

    @pl.when(col > 0)
    def _():
        for j in ORDER:
            to_left(j).wait_send()

    for copy in one + two + three:
        copy.wait_send()


def front(sky, table, flags):
    bf, f32 = jnp.bfloat16, jnp.float32
    dma = pltpu.SemaphoreType.DMA
    return pl.pallas_call(
        front_kernel,
        out_shape=(jax.ShapeDtypeStruct((256, 256, 128), bf), jax.ShapeDtypeStruct((2, 128, 128), f32)),
        in_specs=[pl.BlockSpec(memory_space=pl.ANY)] + [pl.BlockSpec(memory_space=pltpu.VMEM)] * 2,
        out_specs=(pl.BlockSpec(memory_space=pl.ANY), pl.BlockSpec(memory_space=pltpu.VMEM)),
        scratch_shapes=[
            pltpu.VMEM((CHANS, 256 + 2 * HW, 128), bf),
            pltpu.VMEM((4, CHANS, CHUNK, 128), bf),
            pltpu.VMEM((4, CHANS, 16, 128), bf),
            pltpu.VMEM((4, CHANS, 16, 128), bf),
            pltpu.VMEM((4, CHANS, 16, 128), bf),
            pltpu.VMEM((4, CHANS, 16, 128), bf),
            pltpu.VMEM((2, 512, 256), bf),
            pltpu.VMEM((512, 256), bf),
            pltpu.VMEM((4096, 128), f32),
            pltpu.VMEM((4096, 128), f32),
            pltpu.VMEM((2, 32, 256, 128), bf),
            pltpu.VMEM((2, 128, 128), f32),
            pltpu.VMEM((PLANE, 3, 8, 128), f32),
            pltpu.VMEM((PLANE, 3, 8, 128), f32),
            pltpu.VMEM((8, 2, 8, 128), f32),
            pltpu.VMEM((GROUP, 8, 2, 8, 128), f32),
            pltpu.VMEM((PLANE, 2, 8, 128), f32),
            pltpu.VMEM((PLANE, 2, 8, 128), f32),
            dma, dma((2,)), dma((2,)), dma((2, 4)), dma((2, 4)), dma((2,)),
            dma((PLANE,)), dma((PLANE,)), dma((GROUP,)), dma((GROUP,)), dma((PLANE,)), dma((PLANE,)),
        ],
        compiler_params=pltpu.CompilerParams(
            collective_id=1, has_side_effects=True, vmem_limit_bytes=56 * 1024 * 1024),
        name="front",
    )(sky, table, flags)


def weights_of(grams, priors, cheb_t, keep):
    lanes = lax.broadcasted_iota(jnp.int32, (8, 128), 1)
    subs = lax.broadcasted_iota(jnp.int32, (8, 128), 0)
    mats = []
    for band in range(2):
        blocks = []
        for i in range(16):
            block = grams[band][i * 8:i * 8 + 8, :]
            diag = jnp.where(lanes == subs + 8 * i, priors[band], 0.0)
            blocks.append(block / 524288.0 + diag)
        blocks.append(cheb_t)
        mats.append(blocks)
    for k in range(128):
        at, off = k // 8, k % 8
        hit = lanes[0:1, :] == k
        for band in range(2):
            m = mats[band]
            cols = [jnp.broadcast_to(b[:, k:k + 1], (8, 128)) for b in m]
            inv = 1.0 / cols[at][off:off + 1, :]
            line = m[at][off:off + 1, :] * inv
            line = jnp.where(hit, 1.0 - inv, line)
            mats[band] = [b - c * line for b, c in zip(m, cols)]
    out = []
    for band in range(2):
        mixed = mats[band][16] * keep
        kept = cheb_t * keep
        small = lax.dot_general(kept, mixed, (((1,), (1,)), ((), ())), precision=HIGH,
                                preferred_element_type=jnp.float32)
        eye = (lax.broadcasted_iota(jnp.int32, (8, 8), 0) == lax.broadcasted_iota(jnp.int32, (8, 8), 1))
        small = small + jnp.where(eye, 1.0 - keep[:, 0:8], 0.0)
        out.append((small, mixed))
    weights = []
    for small, mixed in out:
        for k in range(8):
            fac = small[:, k:k + 1]
            inv = 1.0 / fac[k:k + 1, :]
            shift = jnp.where(subs[:, 0:1] == k, 1.0, 0.0)
            fac = fac - shift
            srow = small[k:k + 1, :] * inv
            mrow = mixed[k:k + 1, :] * inv
            small = small - fac * srow
            mixed = mixed - fac * mrow
        weights.append(mixed)
    return weights


def back_kernel(gram_ref, prior_ref, cheb_ref, keep_ref, bands_ref, out_ref, proj, flat):
    @pl.when(pl.program_id(0) == 0)
    def _():
        cheb_t = cheb_ref[...]
        keep = keep_ref[...]
        weights = weights_of([gram_ref[0], gram_ref[1]], [prior_ref[0:1, :], prior_ref[1:2, :]], cheb_t, keep)
        kept = cheb_t * keep
        for band in range(2):
            part = lax.dot_general(kept, weights[band], (((0,), (0,)), ((), ())), precision=HIGH,
                                   preferred_element_type=jnp.float32)
            proj[:, 128 * band:128 * band + 128] = part.astype(jnp.bfloat16)

    for y in range(0, 16, 2):
        pair = jnp.concatenate([bands_ref[y], bands_ref[y + 1]], axis=1)
        removed = jnp.dot(proj[...], pair, preferred_element_type=jnp.float32)
        wide = pair.astype(jnp.float32)
        result = wide[0:128] + wide[128:256] - removed
        flat[pl.ds(y, 128, stride=16), :] = result[:, 0:128]
        flat[pl.ds(y + 1, 128, stride=16), :] = result[:, 128:256]
    out_ref[...] = flat[...].reshape(128, 16, 128).astype(jnp.bfloat16)


def back(grams, prior_var, cheb_t, keep, bands):
    whole = pl.BlockSpec(memory_space=pltpu.VMEM)
    return pl.pallas_call(
        back_kernel,
        grid=(16,),
        out_shape=jax.ShapeDtypeStruct((128, 256, 128), jnp.bfloat16),
        in_specs=[whole] * 4 + [pl.BlockSpec((16, 256, 128), lambda i: (i, 0, 0))],
        out_specs=pl.BlockSpec((128, 16, 128), lambda i: (0, i, 0)),
        scratch_shapes=[pltpu.VMEM((128, 256), jnp.bfloat16), pltpu.VMEM((2048, 128), jnp.float32)],
        name="back",
    )(grams, prior_var, cheb_t, keep, bands)


def taps_table(kernel_widths):
    line = lax.broadcasted_iota(jnp.int32, (256, 128), 0)
    lane = lax.broadcasted_iota(jnp.int32, (256, 128), 1)
    first = line < 192
    offsets = jnp.where(first, line - lane - HW, lane - (line - 192) - HW).astype(jnp.float32)
    spread = jnp.where(first, kernel_widths[1], kernel_widths[0]).astype(jnp.float32)
    values = (1.0 + jnp.cos(math.pi * offsets / (spread + 1.0))) / (2.0 * spread + 2.0)
    return jnp.where(jnp.abs(offsets) <= spread, values, 0.0).astype(jnp.bfloat16)


def chebyshev_rows(chan_count, degree):
    position = (2.0 * jnp.arange(chan_count, dtype=jnp.float32) + 1.0) / chan_count - 1.0
    terms = [jnp.ones_like(position), position]
    for order in range(2, degree):
        terms.append(2.0 * position * terms[-1] - terms[-2])
    return jnp.stack(terms[:degree], axis=0)


def local(sky, kernel_widths, prior_var, tile_region, region_rank):
    region = tile_region[0, 0]
    flags = jnp.broadcast_to((jnp.arange(8) == region).astype(jnp.float32)[:, None], (8, 128))
    keep_rank = lax.dynamic_index_in_dim(region_rank, region, 0, keepdims=False)
    keep = jnp.broadcast_to((jnp.arange(8) < keep_rank).astype(jnp.float32)[:, None], (8, 128))
    bands, own_gram = front(sky, taps_table(kernel_widths), flags)
    return back(own_gram, prior_var, chebyshev_rows(sky.shape[0], MMAX), keep, bands)


def solution(mesh):
    return jax.shard_map(
        local,
        mesh=mesh,
        in_specs=(P(None, "row", "col"), P(), P(), P("row", "col"), P()),
        out_specs=P(None, "row", "col"),
        check_vma=False,
    )
```

time: 332 us -> 153 us (0.46); the launches traced: 327 us -> 152 us
  Pallas kernels: 41.7 us -> 142 us
  matrix products: 73.6 us -> 0 us
  other arithmetic: 69.9 us -> 4.63 us
  local copies, waits for them, and re-layouts: 68.5 us -> 4.5 us
  waiting for transfers between devices: 58.1 us -> 0 us
  starting transfers between devices: 12.6 us -> 0 us
    pallas_call x2, Pallas kernels: 41.7 us -> 142 us  [the longest x1 113 us: front(): pl.pallas_call(front_kernel, out_shape=(jax.ShapeDtypeStruct((256, 256, 1...]
    dot_general x5 -> x0, matrix products: 73.6 us -> none  [the longest x1 25.8 us: local(): jnp.einsum('cyx,xz->cyz', smooth, across_table, preferred_element_type=jn...]
    ppermute x4 -> x0, waiting for transfers between devices: 58.1 us -> none  [the longest x2 48.1 us: extended_2(): lax.ppermute(tail, axis, [(i, (i + 1) % count) for i in range(ends)])]
    convert_element_type x2, other arithmetic: 31.7 us -> 1.22 us  [the longest x1 1.22 us: taps_table(): jnp.where(jnp.abs(offsets) <= spread, values, 0.0).astype(jnp.bfloat16)]
    concatenate x1 -> x0, other arithmetic: 29 us -> none  [extended_2(): jnp.concatenate([lax.ppermute(tail, axis, [(i, (i + 1) % count) for i in...]
    concatenate x1 -> x0, local copies, waits for them, and re-layouts: 26.2 us -> none  [extended_2(): jnp.concatenate([lax.ppermute(tail, axis, [(i, (i + 1) % count) for i in...]
    convert_element_type x2 -> x0, local copies, waits for them, and re-layouts: 25.3 us -> none  [the longest x1 12.8 us: local(): coarse = jnp.einsum('cyx,xz->cyz', smooth, across_table, preferred_elemen...]
    unnamed x15 -> x0, local copies, waits for them, and re-layouts: 12.7 us -> none
  transfers between devices with their start and end apart: 4 -> 0, of which waited for: 4 -> 0; matrix products, arithmetic and copies ran while one was open for 1% -> 0% of each run, Pallas kernels for 0% -> 0%
where the time goes in v2:
time: 153 us; the launch traced here: 152 us
  Pallas kernels  142 us (93%)
  other arithmetic  4.63 us (3%)
  local copies, waits for them, and re-layouts  4.5 us (3%)
    pallas_call x1, Pallas kernels, front(): pl.pallas_call(front_kernel, out_shape=(jax.ShapeDtypeStruct((256, 256, 1...  113 us
    pallas_call x1, Pallas kernels, back(): pl.pallas_call(back_kernel, grid=(16,), out_shape=jax.ShapeDtypeStruct((1...  29.6 us

profile of v2, /device:TPU:1, one launch (start us, length us, event | category | flops | bytes accessed | tf_op | source)
XLA Modules:
  0.0 152.1 jit_solution(10209247815373868419)
XLA Ops:
  0.7 1.2 dynamic_slice.4
  1.9 0.6 compare_convert_fusion
  2.6 1.3 fusion.4
  4.0 0.6 stack.2.cheb_ref
  4.6 1.3 multiply_add_fusion
  5.9 1.3 iota_add_fusion
  7.3 0.7 broadcast_in_dim.28.keep_ref
  8.0 0.7 broadcast_in_dim.27.flag_ref
  8.6 1.2 select_convert_fusion.table_ref
  9.8 112.6 %front.1 = (bf16[256,256,128]{2,1,0:T(8,128)(2,1)}, f32[2,128,128]{2,1,0:T(8,128)}) custom-call(bf16[128,256,128]{2,1,0:T(8,128)(2,1)} %sky_ref.1, bf16[256,128]{1,0:T(8,128)(2,1)} %select_convert_fusion.table_ref, f32[8,128]{1,0:T(8,128)} %broadcast_in_dim.27.flag_ref), custom_call_target="tpu_custom_call" | custom-call | tf_op jit(solution)/shard_map/front/pallas_call | solution.py:303
  122.5 29.6 %back.1 = bf16[128,256,128]{2,1,0:T(8,128)(2,1)} custom-call(f32[2,128,128]{2,1,0:T(8,128)} %get-tuple-element.7.gram_ref, f32[2,128]{1,0:T(2,128)} %prior_ref.1, f32[8,128]{1,0:T(8,128)} %stack.2.cheb_ref, f32[8,128]{1,0:T(8,128)} %broadcast_in_dim.28.keep_ref, bf16[256,256,128]{2,1,0:T(8,128)(2,1)} %get-tuple-element.8.bands_ref), custom_call_target="tpu_custom_call" | custom-call | tf_op jit(solution)/shard_map/back/pallas_call | solution.py:406
  (7 shorter events, 0.1 us)

commit v3 on v2

--- a/solution.py
+++ b/solution.py
@@ -19,10 +19,20 @@
 NT = (((1,), (1,)), ((), ()))
 
 
-def front_kernel(sky_ref, table_ref, flag_ref, bands_ref, gram_ref,
-                 skyx, smooth, out_l, out_r, in_l, in_r, across, pick, flat_c, flat_f, stage, grams, pieces,
+def taps_table(down_width, across_width):
+    line = lax.broadcasted_iota(jnp.int32, (256, 128), 0)
+    lane = lax.broadcasted_iota(jnp.int32, (256, 128), 1)
+    first = line < 192
+    offsets = jnp.where(first, line - lane - HW, lane - (line - 192) - HW).astype(jnp.float32)
+    spread = jnp.where(first, across_width, down_width).astype(jnp.float32)
+    values = (1.0 + jnp.cos(math.pi * offsets / (spread + 1.0))) / (2.0 * spread + 2.0)
+    return jnp.where(jnp.abs(offsets) <= spread, values, 0.0).astype(jnp.bfloat16)
+
+
+def front_kernel(widths_ref, region_ref, sky_ref, bands_ref, gram_ref,
+                 table_ref, skyx, smooth, out_l, out_r, in_l, in_r, across, pick, flat_c, flat_f, stage, grams, pieces,
                  first, slots, others, picked, last,
-                 sky_sem, ys, yr, xs, xr, stage_sem, s1, r1, s2, r2, s3, r3):
+                 go, sky_sem, ys, yr, xs, xr, stage_sem, s1, r1, s2, r2, s3, r3):
     row = lax.axis_index("row")
     col = lax.axis_index("col")
     part = lax.rem(col, PLANE)
@@ -46,6 +56,8 @@
 
     load = pltpu.make_async_copy(sky_ref, skyx.at[:, HW:HW + 256, :], sky_sem)
     load.start()
+
+    table_ref[...] = taps_table(widths_ref[0], widths_ref[1])
 
     zero = jnp.zeros((512, 256), jnp.bfloat16)
     own = table_ref[HW:HW + 128, :]
@@ -111,14 +123,43 @@
             device_id=(row, lax.rem(col + 31, 32)), device_id_type=MESH)
 
     for j in ORDER:
-        if j == 0:
+        if j == ORDER[2]:
             @pl.when(row > 0)
             def _():
                 to_next.wait_recv()
-        if j == 3:
+
             @pl.when(row < 3)
             def _():
                 to_last.wait_recv()
+
+            middle = (row == 1) | (row == 2)
+            crossing = (col == 15) | (col == 16)
+
+            @pl.when(middle & (col == 12))
+            def _():
+                pl.semaphore_signal(go, inc=1, device_id=(row, col + 3), device_id_type=MESH)
+
+            @pl.when(middle & (col == 19))
+            def _():
+                pl.semaphore_signal(go, inc=1, device_id=(row, col - 3), device_id_type=MESH)
+
+            @pl.when(crossing)
+            def _():
+                pl.semaphore_wait(go, 1)
+
+            @pl.when(middle & crossing)
+            def _():
+                pl.semaphore_signal(go, inc=1, device_id=((row - 1) * 3, col), device_id_type=MESH)
+
+            @pl.when(col == 15)
+            def _():
+                to_right(ORDER[0]).start()
+                to_right(ORDER[1]).start()
+
+            @pl.when(col == 16)
+            def _():
+                to_left(ORDER[0]).start()
+                to_left(ORDER[1]).start()
 
         def smooth_some(step, carry, j=j):
             c0 = step * 16
@@ -144,11 +185,13 @@
 
         lax.fori_loop(0, 4, pack_some, 0)
 
-        @pl.when(col < 31)
+        late = j in ORDER[2:]
+
+        @pl.when((col < 31) & (late | (col != 15)))
         def _(j=j):
             to_right(j).start()
 
-        @pl.when(col > 0)
+        @pl.when((col > 0) & (late | (col != 16)))
         def _(j=j):
             to_left(j).start()
 
@@ -201,10 +244,11 @@
             lax.fori_loop(0, 2, turn_some, 0)
             put(h, CHUNK * j + 32 * h).start()
 
+    flag = jnp.where(lax.broadcasted_iota(jnp.int32, (8, 128), 0) == region_ref[0, 0], 1.0, 0.0)
     for q in range(PLANE):
         pieces[q, 0] = grams[0, 8 * q:8 * q + 8, :]
         pieces[q, 1] = grams[1, 8 * q:8 * q + 8, :]
-        pieces[q, 2] = flag_ref[...]
+        pieces[q, 2] = flag
     one = []
     for step in range(1, PLANE):
         one.append(pltpu.make_async_remote_copy(
@@ -297,15 +341,16 @@
         copy.wait_send()
 
 
-def front(sky, table, flags):
+def front(widths, region, sky):
     bf, f32 = jnp.bfloat16, jnp.float32
     dma = pltpu.SemaphoreType.DMA
     return pl.pallas_call(
         front_kernel,
         out_shape=(jax.ShapeDtypeStruct((256, 256, 128), bf), jax.ShapeDtypeStruct((2, 128, 128), f32)),
-        in_specs=[pl.BlockSpec(memory_space=pl.ANY)] + [pl.BlockSpec(memory_space=pltpu.VMEM)] * 2,
+        in_specs=[pl.BlockSpec(memory_space=pltpu.SMEM)] * 2 + [pl.BlockSpec(memory_space=pl.ANY)],
         out_specs=(pl.BlockSpec(memory_space=pl.ANY), pl.BlockSpec(memory_space=pltpu.VMEM)),
         scratch_shapes=[
+            pltpu.VMEM((256, 128), bf),
             pltpu.VMEM((CHANS, 256 + 2 * HW, 128), bf),
             pltpu.VMEM((4, CHANS, CHUNK, 128), bf),
             pltpu.VMEM((4, CHANS, 16, 128), bf),
@@ -324,13 +369,14 @@
             pltpu.VMEM((GROUP, 8, 2, 8, 128), f32),
             pltpu.VMEM((PLANE, 2, 8, 128), f32),
             pltpu.VMEM((PLANE, 2, 8, 128), f32),
+            pltpu.SemaphoreType.REGULAR,
             dma, dma((2,)), dma((2,)), dma((2, 4)), dma((2, 4)), dma((2,)),
             dma((PLANE,)), dma((PLANE,)), dma((GROUP,)), dma((GROUP,)), dma((PLANE,)), dma((PLANE,)),
         ],
         compiler_params=pltpu.CompilerParams(
             collective_id=1, has_side_effects=True, vmem_limit_bytes=56 * 1024 * 1024),
         name="front",
-    )(sky, table, flags)
+    )(widths, region, sky)
 
 
 def weights_of(grams, priors, cheb_t, keep):
@@ -379,11 +425,24 @@
     return weights
 
 
-def back_kernel(gram_ref, prior_ref, cheb_ref, keep_ref, bands_ref, out_ref, proj, flat):
+def chebyshev_rows():
+    lane = lax.broadcasted_iota(jnp.int32, (8, 128), 1).astype(jnp.float32)
+    order = lax.broadcasted_iota(jnp.int32, (8, 128), 0)
+    position = (2.0 * lane + 1.0) / CHANS - 1.0
+    terms = [jnp.ones_like(position), position]
+    rows = jnp.where(order == 0, terms[0], position)
+    for m in range(2, MMAX):
+        terms.append(2.0 * position * terms[-1] - terms[-2])
+        rows = jnp.where(order == m, terms[-1], rows)
+    return rows
+
+
+def back_kernel(region_ref, rank_ref, gram_ref, prior_ref, bands_ref, out_ref, proj, flat):
     @pl.when(pl.program_id(0) == 0)
     def _():
-        cheb_t = cheb_ref[...]
-        keep = keep_ref[...]
+        cheb_t = chebyshev_rows()
+        rank = rank_ref[region_ref[0, 0]]
+        keep = jnp.where(lax.broadcasted_iota(jnp.int32, (8, 128), 0) < rank, 1.0, 0.0)
         weights = weights_of([gram_ref[0], gram_ref[1]], [prior_ref[0:1, :], prior_ref[1:2, :]], cheb_t, keep)
         kept = cheb_t * keep
         for band in range(2):
@@ -401,44 +460,22 @@
     out_ref[...] = flat[...].reshape(128, 16, 128).astype(jnp.bfloat16)
 
 
-def back(grams, prior_var, cheb_t, keep, bands):
+def back(region, ranks, grams, prior_var, bands):
     whole = pl.BlockSpec(memory_space=pltpu.VMEM)
     return pl.pallas_call(
         back_kernel,
         grid=(16,),
         out_shape=jax.ShapeDtypeStruct((128, 256, 128), jnp.bfloat16),
-        in_specs=[whole] * 4 + [pl.BlockSpec((16, 256, 128), lambda i: (i, 0, 0))],
+        in_specs=[pl.BlockSpec(memory_space=pltpu.SMEM)] * 2 + [whole] * 2 + [pl.BlockSpec((16, 256, 128), lambda i: (i, 0, 0))],
         out_specs=pl.BlockSpec((128, 16, 128), lambda i: (0, i, 0)),
         scratch_shapes=[pltpu.VMEM((128, 256), jnp.bfloat16), pltpu.VMEM((2048, 128), jnp.float32)],
         name="back",
-    )(grams, prior_var, cheb_t, keep, bands)
-
-
-def taps_table(kernel_widths):
-    line = lax.broadcasted_iota(jnp.int32, (256, 128), 0)
-    lane = lax.broadcasted_iota(jnp.int32, (256, 128), 1)
-    first = line < 192
-    offsets = jnp.where(first, line - lane - HW, lane - (line - 192) - HW).astype(jnp.float32)
-    spread = jnp.where(first, kernel_widths[1], kernel_widths[0]).astype(jnp.float32)
-    values = (1.0 + jnp.cos(math.pi * offsets / (spread + 1.0))) / (2.0 * spread + 2.0)
-    return jnp.where(jnp.abs(offsets) <= spread, values, 0.0).astype(jnp.bfloat16)
-
-
-def chebyshev_rows(chan_count, degree):
-    position = (2.0 * jnp.arange(chan_count, dtype=jnp.float32) + 1.0) / chan_count - 1.0
-    terms = [jnp.ones_like(position), position]
-    for order in range(2, degree):
-        terms.append(2.0 * position * terms[-1] - terms[-2])
-    return jnp.stack(terms[:degree], axis=0)
+    )(region, ranks, grams, prior_var, bands)
 
 
 def local(sky, kernel_widths, prior_var, tile_region, region_rank):
-    region = tile_region[0, 0]
-    flags = jnp.broadcast_to((jnp.arange(8) == region).astype(jnp.float32)[:, None], (8, 128))
-    keep_rank = lax.dynamic_index_in_dim(region_rank, region, 0, keepdims=False)
-    keep = jnp.broadcast_to((jnp.arange(8) < keep_rank).astype(jnp.float32)[:, None], (8, 128))
-    bands, own_gram = front(sky, taps_table(kernel_widths), flags)
-    return back(own_gram, prior_var, chebyshev_rows(sky.shape[0], MMAX), keep, bands)
+    bands, own_gram = front(kernel_widths, tile_region, sky)
+    return back(tile_region, region_rank, own_gram, prior_var, bands)
 
 
 def solution(mesh):

time: 153 us -> 131 us (0.86)
  Pallas kernels: 142 us -> 130 us
  other arithmetic: 4.63 us -> 0 us
  local copies, waits for them, and re-layouts: 4.5 us -> 0 us
    pallas_call x1, Pallas kernels: 113 us -> 99.8 us  [front(): pl.pallas_call(front_kernel, out_shape=(jax.ShapeDtypeStruct((256, 256, 1...]
    convert_element_type x3 -> x0, other arithmetic: 1.87 us -> none  [the longest x1 1.22 us: taps_table(): jnp.where(jnp.abs(offsets) <= spread, values, 0.0).astype(jnp.bfloat16)]
where the time goes in v3:
time: 131 us; the launch traced here: 130 us
  Pallas kernels  130 us (99%)
    pallas_call x1, Pallas kernels, front(): pl.pallas_call(front_kernel, out_shape=(jax.ShapeDtypeStruct((256, 256, 1...  99.8 us
    pallas_call x1, Pallas kernels, back(): pl.pallas_call(back_kernel, grid=(16,), out_shape=jax.ShapeDtypeStruct((1...  29.8 us

profile of v3, /device:TPU:1, one launch (start us, length us, event | category | flops | bytes accessed | tf_op | source)
XLA Modules:
  0.0 130.2 jit_solution(9851678469155394693)
XLA Ops:
  0.7 99.8 %front.1 = (bf16[256,256,128]{2,1,0:T(8,128)(2,1)}, f32[2,128,128]{2,1,0:T(8,128)}) custom-call(s32[2]{0:T(128)} %widths_ref.1, s32[1,1]{1,0:T(1,128)S(6)} %copy.6.region_ref, bf16[128,256,128]{2,1,0:T(8,128)(2,1)} %sky_ref.1), custom_call_target="tpu_custom_call" | custom-call | tf_op jit(solution)/shard_map/front/pallas_call | solution.py:347
  100.4 29.8 %back.1 = bf16[128,256,128]{2,1,0:T(8,128)(2,1)} custom-call(s32[1,1]{1,0:T(1,128)S(6)} %copy.6.region_ref, s32[8]{0:T(128)} %rank_ref.1, f32[2,128,128]{2,1,0:T(8,128)} %get-tuple-element.7.gram_ref, f32[2,128]{1,0:T(2,128)} %prior_ref.1, bf16[256,256,128]{2,1,0:T(8,128)(2,1)} %get-tuple-element.8.bands_ref), custom_call_target="tpu_custom_call" | custom-call | tf_op jit(solution)/shard_map/back/pallas_call | solution.py:465

commit v4 on v3

--- a/solution.py
+++ b/solution.py
@@ -30,9 +30,9 @@
 
 
 def front_kernel(widths_ref, region_ref, sky_ref, bands_ref, gram_ref,
-                 table_ref, skyx, smooth, out_l, out_r, in_l, in_r, across, pick, flat_c, flat_f, stage, grams, pieces,
+                 table_ref, skyx, smooth, out_l, out_r, in_l, in_r, across, pick, flat_c, flat_f, grams, pieces,
                  first, slots, others, picked, last,
-                 go, sky_sem, ys, yr, xs, xr, stage_sem, s1, r1, s2, r2, s3, r3):
+                 go, sky_sem, ys, yr, xs, xr, s1, r1, s2, r2, s3, r3):
     row = lax.axis_index("row")
     col = lax.axis_index("col")
     part = lax.rem(col, PLANE)
@@ -93,8 +93,6 @@
     def _():
         in_r[...] = jnp.zeros(in_r.shape, jnp.bfloat16)
 
-    pl.semaphore_wait(barrier, PLANE + GROUP)
-
     to_next = pltpu.make_async_remote_copy(
         src_ref=sky_ref.at[:, 256 - HW:256, :], dst_ref=skyx.at[:, 0:HW, :],
         send_sem=ys.at[0], recv_sem=yr.at[0], device_id=(lax.rem(row + 1, 4), col), device_id_type=MESH)
@@ -102,16 +100,6 @@
         src_ref=sky_ref.at[:, 0:HW, :], dst_ref=skyx.at[:, HW + 256:, :],
         send_sem=ys.at[1], recv_sem=yr.at[1], device_id=(lax.rem(row + 3, 4), col), device_id_type=MESH)
 
-    @pl.when(row < 3)
-    def _():
-        to_next.start()
-
-    @pl.when(row > 0)
-    def _():
-        to_last.start()
-
-    load.wait()
-
     def to_right(j):
         return pltpu.make_async_remote_copy(
             src_ref=out_r.at[j], dst_ref=in_l.at[j], send_sem=xs.at[0, j], recv_sem=xr.at[0, j],
@@ -122,46 +110,8 @@
             src_ref=out_l.at[j], dst_ref=in_r.at[j], send_sem=xs.at[1, j], recv_sem=xr.at[1, j],
             device_id=(row, lax.rem(col + 31, 32)), device_id_type=MESH)
 
-    for j in ORDER:
-        if j == ORDER[2]:
-            @pl.when(row > 0)
-            def _():
-                to_next.wait_recv()
-
-            @pl.when(row < 3)
-            def _():
-                to_last.wait_recv()
-
-            middle = (row == 1) | (row == 2)
-            crossing = (col == 15) | (col == 16)
-
-            @pl.when(middle & (col == 12))
-            def _():
-                pl.semaphore_signal(go, inc=1, device_id=(row, col + 3), device_id_type=MESH)
-
-            @pl.when(middle & (col == 19))
-            def _():
-                pl.semaphore_signal(go, inc=1, device_id=(row, col - 3), device_id_type=MESH)
-
-            @pl.when(crossing)
-            def _():
-                pl.semaphore_wait(go, 1)
-
-            @pl.when(middle & crossing)
-            def _():
-                pl.semaphore_signal(go, inc=1, device_id=((row - 1) * 3, col), device_id_type=MESH)
-
-            @pl.when(col == 15)
-            def _():
-                to_right(ORDER[0]).start()
-                to_right(ORDER[1]).start()
-
-            @pl.when(col == 16)
-            def _():
-                to_left(ORDER[0]).start()
-                to_left(ORDER[1]).start()
-
-        def smooth_some(step, carry, j=j):
+    def smooth_chunk(j):
+        def smooth_some(step, carry):
             c0 = step * 16
             for p in range(8):
                 c = c0 + 2 * p
@@ -174,7 +124,8 @@
 
         lax.fori_loop(0, 8, smooth_some, 0)
 
-        def pack_some(step, carry, j=j):
+    def pack_chunk(j):
+        def pack_some(step, carry):
             c0 = step * 32
             wide = jnp.concatenate(
                 [smooth[j, pl.ds(c0, 32), 16 * q:16 * q + 16, :].reshape(512, 128) for q in range(4)], axis=1)
@@ -185,7 +136,58 @@
 
         lax.fori_loop(0, 4, pack_some, 0)
 
-        late = j in ORDER[2:]
+    load.wait()
+    for j in ORDER:
+        if j == ORDER[2]:
+            @pl.when(row > 0)
+            def _():
+                to_next.wait_recv()
+
+            @pl.when(row < 3)
+            def _():
+                to_last.wait_recv()
+
+            middle = (row == 1) | (row == 2)
+            crossing = (col == 15) | (col == 16)
+
+            @pl.when(middle & (col == 12))
+            def _():
+                pl.semaphore_signal(go, inc=1, device_id=(row, col + 3), device_id_type=MESH)
+
+            @pl.when(middle & (col == 19))
+            def _():
+                pl.semaphore_signal(go, inc=1, device_id=(row, col - 3), device_id_type=MESH)
+
+            @pl.when(crossing)
+            def _():
+                pl.semaphore_wait(go, 1)
+
+            @pl.when(middle & crossing)
+            def _():
+                pl.semaphore_signal(go, inc=1, device_id=((row - 1) * 3, col), device_id_type=MESH)
+
+            @pl.when(col == 15)
+            def _():
+                to_right(ORDER[1]).start()
+
+            @pl.when(col == 16)
+            def _():
+                to_left(ORDER[1]).start()
+
+        smooth_chunk(j)
+        if j == ORDER[0]:
+            pl.semaphore_wait(barrier, PLANE + GROUP)
+
+            @pl.when(row < 3)
+            def _():
+                to_next.start()
+
+            @pl.when(row > 0)
+            def _():
+                to_last.start()
+
+        pack_chunk(j)
+        late = j != ORDER[1]
 
         @pl.when((col < 31) & (late | (col != 15)))
         def _(j=j):
@@ -195,10 +197,7 @@
         def _(j=j):
             to_left(j).start()
 
-    def put(h, base):
-        return pltpu.make_async_copy(stage.at[h], bands_ref.at[pl.ds(base, 32)], stage_sem.at[h])
-
-    for turn, j in enumerate(ORDER):
+    for j in ORDER:
         @pl.when(col > 0)
         def _(j=j):
             to_right(j).wait_recv()
@@ -225,16 +224,14 @@
                 return carry
 
             lax.fori_loop(0, 4, coarse_some, 0)
-            if turn > 0:
-                put(h, 0).wait()
-
-            def turn_some(k, carry, h=h):
+
+            def turn_some(k, carry, j=j, h=h):
                 for y0 in range(0, 16, 4):
                     for band, flat in ((0, flat_c), (1, flat_f)):
                         lines = []
                         for y in range(y0, y0 + 4):
                             line = flat[pl.ds(2048 * k + y, 128, stride=16), :].astype(jnp.bfloat16)
-                            stage[h, 16 * k + y, 128 * band:128 * band + 128, :] = line
+                            bands_ref[CHUNK * j + 32 * h + 16 * k + y, 128 * band:128 * band + 128, :] = line
                             lines.append(line)
                         wide = jnp.concatenate(lines, axis=1)
                         grams[band] = grams[band] + lax.dot_general(
@@ -242,7 +239,6 @@
                 return carry
 
             lax.fori_loop(0, 2, turn_some, 0)
-            put(h, CHUNK * j + 32 * h).start()
 
     flag = jnp.where(lax.broadcasted_iota(jnp.int32, (8, 128), 0) == region_ref[0, 0], 1.0, 0.0)
     for q in range(PLANE):
@@ -316,9 +312,6 @@
         for band in range(2):
             gram_ref[band, index * 8:index * 8 + 8, :] = last[index, band]
 
-    for h in range(2):
-        put(h, 0).wait()
-
     @pl.when(row < 3)
     def _():
         to_next.wait_send()
@@ -346,9 +339,9 @@
     dma = pltpu.SemaphoreType.DMA
     return pl.pallas_call(
         front_kernel,
-        out_shape=(jax.ShapeDtypeStruct((256, 256, 128), bf), jax.ShapeDtypeStruct((2, 128, 128), f32)),
+        out_shape=(pltpu.VMEM((256, 256, 128), bf), pltpu.VMEM((2, 128, 128), f32)),
         in_specs=[pl.BlockSpec(memory_space=pltpu.SMEM)] * 2 + [pl.BlockSpec(memory_space=pl.ANY)],
-        out_specs=(pl.BlockSpec(memory_space=pl.ANY), pl.BlockSpec(memory_space=pltpu.VMEM)),
+        out_specs=(pl.BlockSpec(memory_space=pltpu.VMEM), pl.BlockSpec(memory_space=pltpu.VMEM)),
         scratch_shapes=[
             pltpu.VMEM((256, 128), bf),
             pltpu.VMEM((CHANS, 256 + 2 * HW, 128), bf),
@@ -361,7 +354,6 @@
             pltpu.VMEM((512, 256), bf),
             pltpu.VMEM((4096, 128), f32),
             pltpu.VMEM((4096, 128), f32),
-            pltpu.VMEM((2, 32, 256, 128), bf),
             pltpu.VMEM((2, 128, 128), f32),
             pltpu.VMEM((PLANE, 3, 8, 128), f32),
             pltpu.VMEM((PLANE, 3, 8, 128), f32),
@@ -370,11 +362,11 @@
             pltpu.VMEM((PLANE, 2, 8, 128), f32),
             pltpu.VMEM((PLANE, 2, 8, 128), f32),
             pltpu.SemaphoreType.REGULAR,
-            dma, dma((2,)), dma((2,)), dma((2, 4)), dma((2, 4)), dma((2,)),
+            dma, dma((2,)), dma((2,)), dma((2, 4)), dma((2, 4)),
             dma((PLANE,)), dma((PLANE,)), dma((GROUP,)), dma((GROUP,)), dma((PLANE,)), dma((PLANE,)),
         ],
         compiler_params=pltpu.CompilerParams(
-            collective_id=1, has_side_effects=True, vmem_limit_bytes=56 * 1024 * 1024),
+            collective_id=1, has_side_effects=True, vmem_limit_bytes=40 * 1024 * 1024),
         name="front",
     )(widths, region, sky)
 
@@ -437,38 +429,55 @@
     return rows
 
 
-def back_kernel(region_ref, rank_ref, gram_ref, prior_ref, bands_ref, out_ref, proj, flat):
-    @pl.when(pl.program_id(0) == 0)
-    def _():
-        cheb_t = chebyshev_rows()
-        rank = rank_ref[region_ref[0, 0]]
-        keep = jnp.where(lax.broadcasted_iota(jnp.int32, (8, 128), 0) < rank, 1.0, 0.0)
-        weights = weights_of([gram_ref[0], gram_ref[1]], [prior_ref[0:1, :], prior_ref[1:2, :]], cheb_t, keep)
-        kept = cheb_t * keep
-        for band in range(2):
-            part = lax.dot_general(kept, weights[band], (((0,), (0,)), ((), ())), precision=HIGH,
-                                   preferred_element_type=jnp.float32)
-            proj[:, 128 * band:128 * band + 128] = part.astype(jnp.bfloat16)
-
-    for y in range(0, 16, 2):
-        pair = jnp.concatenate([bands_ref[y], bands_ref[y + 1]], axis=1)
-        removed = jnp.dot(proj[...], pair, preferred_element_type=jnp.float32)
-        wide = pair.astype(jnp.float32)
-        result = wide[0:128] + wide[128:256] - removed
-        flat[pl.ds(y, 128, stride=16), :] = result[:, 0:128]
-        flat[pl.ds(y + 1, 128, stride=16), :] = result[:, 128:256]
-    out_ref[...] = flat[...].reshape(128, 16, 128).astype(jnp.bfloat16)
+def back_kernel(region_ref, rank_ref, gram_ref, prior_ref, bands_ref, out_ref, proj, flat, ready, sems):
+    cheb_t = chebyshev_rows()
+    rank = rank_ref[region_ref[0, 0]]
+    keep = jnp.where(lax.broadcasted_iota(jnp.int32, (8, 128), 0) < rank, 1.0, 0.0)
+    weights = weights_of([gram_ref[0], gram_ref[1]], [prior_ref[0:1, :], prior_ref[1:2, :]], cheb_t, keep)
+    kept = cheb_t * keep
+    for band in range(2):
+        part = lax.dot_general(kept, weights[band], (((0,), (0,)), ((), ())), precision=HIGH,
+                               preferred_element_type=jnp.float32)
+        proj[:, 128 * band:128 * band + 128] = part.astype(jnp.bfloat16)
+
+    def put(slot, base):
+        return pltpu.make_async_copy(ready.at[slot], out_ref.at[:, pl.ds(base, 16), :], sems.at[slot])
+
+    def block(step, carry):
+        for slot in range(2):
+            base = pl.multiple_of(step * 32 + slot * 16, 16)
+            for y in range(0, 16, 2):
+                pair = jnp.concatenate([bands_ref[base + y], bands_ref[base + y + 1]], axis=1)
+                removed = jnp.dot(proj[...], pair, preferred_element_type=jnp.float32)
+                wide = pair.astype(jnp.float32)
+                result = wide[0:128] + wide[128:256] - removed
+                flat[pl.ds(2048 * slot + y, 128, stride=16), :] = result[:, 0:128]
+                flat[pl.ds(2048 * slot + y + 1, 128, stride=16), :] = result[:, 128:256]
+
+            @pl.when(step > 0)
+            def _(slot=slot):
+                put(slot, 0).wait()
+
+            ready[slot] = flat[2048 * slot:2048 * slot + 2048, :].reshape(128, 16, 128).astype(jnp.bfloat16)
+            put(slot, base).start()
+        return carry
+
+    lax.fori_loop(0, 8, block, 0)
+    put(0, 0).wait()
+    put(1, 0).wait()
 
 
 def back(region, ranks, grams, prior_var, bands):
     whole = pl.BlockSpec(memory_space=pltpu.VMEM)
+    bands = pltpu.with_memory_space_constraint(bands, pltpu.VMEM)
     return pl.pallas_call(
         back_kernel,
-        grid=(16,),
         out_shape=jax.ShapeDtypeStruct((128, 256, 128), jnp.bfloat16),
-        in_specs=[pl.BlockSpec(memory_space=pltpu.SMEM)] * 2 + [whole] * 2 + [pl.BlockSpec((16, 256, 128), lambda i: (i, 0, 0))],
-        out_specs=pl.BlockSpec((128, 16, 128), lambda i: (0, i, 0)),
-        scratch_shapes=[pltpu.VMEM((128, 256), jnp.bfloat16), pltpu.VMEM((2048, 128), jnp.float32)],
+        in_specs=[pl.BlockSpec(memory_space=pltpu.SMEM)] * 2 + [whole] * 3,
+        out_specs=pl.BlockSpec(memory_space=pl.ANY),
+        scratch_shapes=[pltpu.VMEM((128, 256), jnp.bfloat16), pltpu.VMEM((4096, 128), jnp.float32),
+                        pltpu.VMEM((2, 128, 16, 128), jnp.bfloat16), pltpu.SemaphoreType.DMA((2,))],
+        compiler_params=pltpu.CompilerParams(vmem_limit_bytes=16 * 1024 * 1024),
         name="back",
     )(region, ranks, grams, prior_var, bands)
 

time: 131 us -> 126 us (0.962)
  Pallas kernels: 130 us -> 124 us
    pallas_call x2, Pallas kernels: 130 us -> 124 us  [the longest x1 101 us: front(): pl.pallas_call(front_kernel, out_shape=(pltpu.VMEM((256, 256, 128), bf),...]
where the time goes in v4:
time: 126 us; the launch traced here: 125 us
  Pallas kernels  124 us (98%)
    pallas_call x1, Pallas kernels, front(): pl.pallas_call(front_kernel, out_shape=(pltpu.VMEM((256, 256, 128), bf),...  101 us
    pallas_call x1, Pallas kernels, back(): pl.pallas_call(back_kernel, out_shape=jax.ShapeDtypeStruct((128, 256, 128...  23.4 us

profile of v4, /device:TPU:1, one launch (start us, length us, event | category | flops | bytes accessed | tf_op | source)
XLA Modules:
  0.0 125.4 jit_solution(3003129698136105635)
XLA Ops:
  0.0 0.0 copy-start.1
  0.0 0.0 copy-start
  0.7 101.1 %front.1 = (bf16[256,256,128]{2,1,0:T(8,128)(2,1)S(1)}, f32[2,128,128]{2,1,0:T(8,128)S(1)}) custom-call(s32[2]{0:T(128)} %widths_ref.1, s32[1,1]{1,0:T(1,128)S(6)} %copy.6.region_ref, bf16[128,256,128]{2,1,0:T(8,128)(2,1)} %sky_ref.1), custom_call_target="tpu_custom_call" | custom-call | tf_op jit(solution)/shard_map/front/pallas_call | solution.py:340
  101.8 0.0 copy-done.1
  101.8 0.0 copy-done
  101.8 23.4 %back.1 = bf16[128,256,128]{2,1,0:T(8,128)(2,1)} custom-call(s32[1,1]{1,0:T(1,128)S(6)} %copy.6.region_ref, s32[8]{0:T(128)S(1)} %copy-done.1, f32[2,128,128]{2,1,0:T(8,128)S(1)} %get-tuple-element.7.gram_ref, f32[2,128]{1,0:T(2,128)S(1)} %copy-done, bf16[256,256,128]{2,1,0:T(8,128)(2,1)S(1)} %get-tuple-element.8.bands_ref), custom_call_target="tpu_custom_call" | custom-call | tf_op jit(solution)/shard_map/back/pallas_call | solution.py:473
Async XLA Ops:
  0.0 101.8 %copy-start.1 = (s32[8]{0:T(128)S(1)}, s32[8]{0:T(128)}, u32[]{:S(2)}) copy-start(s32[8]{0:T(128)} %rank_ref.1) | copy-start | bytes 100
  0.0 101.8 %copy-start = (f32[2,128]{1,0:T(2,128)S(1)}, f32[2,128]{1,0:T(2,128)}, u32[]{:S(2)}) copy-start(f32[2,128]{1,0:T(2,128)} %prior_ref.1) | copy-start | bytes 3076

commit v5 on v4

--- a/solution.py
+++ b/solution.py
@@ -13,7 +13,6 @@
 GROUP = 8
 CHANS = 128
 CHUNK = 64
-ORDER = (1, 2, 0, 3)
 MESH = pl.DeviceIdType.MESH
 HIGH = lax.Precision.HIGHEST
 NT = (((1,), (1,)), ((), ()))
@@ -32,7 +31,7 @@
 def front_kernel(widths_ref, region_ref, sky_ref, bands_ref, gram_ref,
                  table_ref, skyx, smooth, out_l, out_r, in_l, in_r, across, pick, flat_c, flat_f, grams, pieces,
                  first, slots, others, picked, last,
-                 go, sky_sem, ys, yr, xs, xr, s1, r1, s2, r2, s3, r3):
+                 sky_sem, ys, yr, xs, xr, s1, r1, s2, r2, s3, r3):
     row = lax.axis_index("row")
     col = lax.axis_index("col")
     part = lax.rem(col, PLANE)
@@ -111,12 +110,14 @@
             device_id=(row, lax.rem(col + 31, 32)), device_id_type=MESH)
 
     def smooth_chunk(j):
+        start = pl.multiple_of(CHUNK * j, CHUNK)
+
         def smooth_some(step, carry):
             c0 = step * 16
             for p in range(8):
                 c = c0 + 2 * p
                 window = jnp.concatenate(
-                    [skyx[c, CHUNK * j:CHUNK * j + 128, :], skyx[c + 1, CHUNK * j:CHUNK * j + 128, :]], axis=1)
+                    [skyx[c, pl.ds(start, 128), :], skyx[c + 1, pl.ds(start, 128), :]], axis=1)
                 result = jnp.dot(down, window, preferred_element_type=jnp.float32).astype(jnp.bfloat16)
                 smooth[j, c] = result[:, 0:128]
                 smooth[j, c + 1] = result[:, 128:256]
@@ -137,45 +138,28 @@
         lax.fori_loop(0, 4, pack_some, 0)
 
     load.wait()
-    for j in ORDER:
-        if j == ORDER[2]:
-            @pl.when(row > 0)
+    order = (1, 2, jnp.where(row == 2, 3, 0), jnp.where(row == 2, 0, 3))
+    for turn, j in enumerate(order):
+        if turn == 2:
+            @pl.when((row == 1) | (row == 3))
             def _():
                 to_next.wait_recv()
 
-            @pl.when(row < 3)
+            @pl.when(row == 2)
             def _():
                 to_last.wait_recv()
 
-            middle = (row == 1) | (row == 2)
-            crossing = (col == 15) | (col == 16)
-
-            @pl.when(middle & (col == 12))
+        if turn == 3:
+            @pl.when((row == 0) | (row == 1))
             def _():
-                pl.semaphore_signal(go, inc=1, device_id=(row, col + 3), device_id_type=MESH)
-
-            @pl.when(middle & (col == 19))
+                to_last.wait_recv()
+
+            @pl.when(row == 2)
             def _():
-                pl.semaphore_signal(go, inc=1, device_id=(row, col - 3), device_id_type=MESH)
-
-            @pl.when(crossing)
-            def _():
-                pl.semaphore_wait(go, 1)
-
-            @pl.when(middle & crossing)
-            def _():
-                pl.semaphore_signal(go, inc=1, device_id=((row - 1) * 3, col), device_id_type=MESH)
-
-            @pl.when(col == 15)
-            def _():
-                to_right(ORDER[1]).start()
-
-            @pl.when(col == 16)
-            def _():
-                to_left(ORDER[1]).start()
+                to_next.wait_recv()
 
         smooth_chunk(j)
-        if j == ORDER[0]:
+        if turn == 0:
             pl.semaphore_wait(barrier, PLANE + GROUP)
 
             @pl.when(row < 3)
@@ -187,17 +171,16 @@
                 to_last.start()
 
         pack_chunk(j)
-        late = j != ORDER[1]
-
-        @pl.when((col < 31) & (late | (col != 15)))
+
+        @pl.when(col < 31)
         def _(j=j):
             to_right(j).start()
 
-        @pl.when((col > 0) & (late | (col != 16)))
+        @pl.when(col > 0)
         def _(j=j):
             to_left(j).start()
 
-    for j in ORDER:
+    for j in order:
         @pl.when(col > 0)
         def _(j=j):
             to_right(j).wait_recv()
@@ -216,9 +199,9 @@
                 both = jnp.dot(wide, across[h], preferred_element_type=jnp.float32)
                 both = both.astype(jnp.bfloat16).astype(jnp.float32)
                 for k in range(2):
-                    begin = HW + CHUNK * j + 32 * h + 16 * k
+                    begin = pl.multiple_of(HW + CHUNK * j + 32 * h + 16 * k, 16)
                     value = both[:, 128 * k:128 * k + 128]
-                    pixels = skyx[pl.ds(c0, 32), begin:begin + 16, :].reshape(512, 128).astype(jnp.float32)
+                    pixels = skyx[pl.ds(c0, 32), pl.ds(begin, 16), :].reshape(512, 128).astype(jnp.float32)
                     flat_c[pl.ds(2048 * k + c0 * 16, 512), :] = value
                     flat_f[pl.ds(2048 * k + c0 * 16, 512), :] = pixels - value
                 return carry
@@ -322,12 +305,12 @@
 
     @pl.when(col < 31)
     def _():
-        for j in ORDER:
+        for j in range(4):
             to_right(j).wait_send()
 
     @pl.when(col > 0)
     def _():
-        for j in ORDER:
+        for j in range(4):
             to_left(j).wait_send()
 
     for copy in one + two + three:
@@ -361,7 +344,6 @@
             pltpu.VMEM((GROUP, 8, 2, 8, 128), f32),
             pltpu.VMEM((PLANE, 2, 8, 128), f32),
             pltpu.VMEM((PLANE, 2, 8, 128), f32),
-            pltpu.SemaphoreType.REGULAR,
             dma, dma((2,)), dma((2,)), dma((2, 4)), dma((2, 4)),
             dma((PLANE,)), dma((PLANE,)), dma((GROUP,)), dma((GROUP,)), dma((PLANE,)), dma((PLANE,)),
         ],
@@ -369,6 +351,9 @@
             collective_id=1, has_side_effects=True, vmem_limit_bytes=40 * 1024 * 1024),
         name="front",
     )(widths, region, sky)
+
+
+WIDE = 4
 
 
 def weights_of(grams, priors, cheb_t, keep):
@@ -383,16 +368,35 @@
             blocks.append(block / 524288.0 + diag)
         blocks.append(cheb_t)
         mats.append(blocks)
-    for k in range(128):
+    for k in range(0, 128, WIDE):
         at, off = k // 8, k % 8
-        hit = lanes[0:1, :] == k
         for band in range(2):
             m = mats[band]
-            cols = [jnp.broadcast_to(b[:, k:k + 1], (8, 128)) for b in m]
-            inv = 1.0 / cols[at][off:off + 1, :]
-            line = m[at][off:off + 1, :] * inv
-            line = jnp.where(hit, 1.0 - inv, line)
-            mats[band] = [b - c * line for b, c in zip(m, cols)]
+            cols = [[jnp.broadcast_to(b[:, k + p:k + p + 1], (8, 128)) for b in m] for p in range(WIDE)]
+            hit = (lanes >= k) & (lanes < k + WIDE)
+            rows = [jnp.where(hit[0:1], jnp.where(lanes[0:1] == k + i, -1.0, 0.0), m[at][off + i:off + i + 1, :])
+                    for i in range(WIDE)]
+            d = [[cols[p][at][off + i:off + i + 1, :] for p in range(WIDE)] for i in range(WIDE)]
+            inv = []
+            for i in range(WIDE):
+                inv.append(1.0 / d[i][i])
+                for l in range(i + 1, WIDE):
+                    t = d[l][i] * inv[i]
+                    rows[l] = rows[l] - t * rows[i]
+                    for j in range(i + 1, WIDE):
+                        d[l][j] = d[l][j] - t * d[i][j]
+            for i in reversed(range(WIDE)):
+                line = rows[i]
+                for j in range(i + 1, WIDE):
+                    line = line - d[i][j] * rows[j]
+                rows[i] = line * inv[i]
+            fresh = []
+            for index, b in enumerate(m):
+                b = jnp.where(hit, 0.0, b)
+                for p in range(WIDE):
+                    b = b - cols[p][index] * rows[p]
+                fresh.append(b)
+            mats[band] = fresh
     out = []
     for band in range(2):
         mixed = mats[band][16] * keep

time: 126 us -> 131 us (1.040)
  Pallas kernels: 124 us -> 130 us
    pallas_call x1, Pallas kernels: 101 us -> 111 us  [front(): pl.pallas_call(front_kernel, out_shape=(pltpu.VMEM((256, 256, 128), bf),...]
    pallas_call x1, Pallas kernels: 23.4 us -> 18.9 us  [back(): pl.pallas_call(back_kernel, out_shape=jax.ShapeDtypeStruct((128, 256, 128...]
where the time goes in v5:
time: 131 us
  Pallas kernels  130 us (99%)
    pallas_call x1, Pallas kernels, front(): pl.pallas_call(front_kernel, out_shape=(pltpu.VMEM((256, 256, 128), bf),...  111 us
    pallas_call x1, Pallas kernels, back(): pl.pallas_call(back_kernel, out_shape=jax.ShapeDtypeStruct((128, 256, 128...  18.9 us

profile of v5, /device:TPU:1, one launch (start us, length us, event | category | flops | bytes accessed | tf_op | source)
XLA Modules:
  0.0 130.9 jit_solution(9095305759335062100)
XLA Ops:
  0.0 0.0 copy-start.1
  0.0 0.0 copy-start
  0.7 111.2 %front.1 = (bf16[256,256,128]{2,1,0:T(8,128)(2,1)S(1)}, f32[2,128,128]{2,1,0:T(8,128)S(1)}) custom-call(s32[2]{0:T(128)} %widths_ref.1, s32[1,1]{1,0:T(1,128)S(6)} %copy.6.region_ref, bf16[128,256,128]{2,1,0:T(8,128)(2,1)} %sky_ref.1), custom_call_target="tpu_custom_call" | custom-call | tf_op jit(solution)/shard_map/front/pallas_call | solution.py:323
  111.8 0.0 copy-done.1
  111.9 0.0 copy-done
  111.9 18.9 %back.1 = bf16[128,256,128]{2,1,0:T(8,128)(2,1)} custom-call(s32[1,1]{1,0:T(1,128)S(6)} %copy.6.region_ref, s32[8]{0:T(128)S(1)} %copy-done.1, f32[2,128,128]{2,1,0:T(8,128)S(1)} %get-tuple-element.7.gram_ref, f32[2,128]{1,0:T(2,128)S(1)} %copy-done, bf16[256,256,128]{2,1,0:T(8,128)(2,1)S(1)} %get-tuple-element.8.bands_ref), custom_call_target="tpu_custom_call" | custom-call | tf_op jit(solution)/shard_map/back/pallas_call | solution.py:477
Async XLA Ops:
  0.0 111.9 %copy-start.1 = (s32[8]{0:T(128)S(1)}, s32[8]{0:T(128)}, u32[]{:S(2)}) copy-start(s32[8]{0:T(128)} %rank_ref.1) | copy-start | bytes 100
  0.0 111.9 %copy-start = (f32[2,128]{1,0:T(2,128)S(1)}, f32[2,128]{1,0:T(2,128)}, u32[]{:S(2)}) copy-start(f32[2,128]{1,0:T(2,128)} %prior_ref.1) | copy-start | bytes 3076

commit v6 on v5

--- a/solution.py
+++ b/solution.py
@@ -31,7 +31,7 @@
 def front_kernel(widths_ref, region_ref, sky_ref, bands_ref, gram_ref,
                  table_ref, skyx, smooth, out_l, out_r, in_l, in_r, across, pick, flat_c, flat_f, grams, pieces,
                  first, slots, others, picked, last,
-                 sky_sem, ys, yr, xs, xr, s1, r1, s2, r2, s3, r3):
+                 go, sky_sem, ys, yr, xs, xr, s1, r1, s2, r2, s3, r3):
     row = lax.axis_index("row")
     col = lax.axis_index("col")
     part = lax.rem(col, PLANE)
@@ -138,6 +138,8 @@
         lax.fori_loop(0, 4, pack_some, 0)
 
     load.wait()
+    middle = (row == 1) | (row == 2)
+    crossing = (col == 15) | (col == 16)
     order = (1, 2, jnp.where(row == 2, 3, 0), jnp.where(row == 2, 0, 3))
     for turn, j in enumerate(order):
         if turn == 2:
@@ -158,6 +160,14 @@
             def _():
                 to_next.wait_recv()
 
+            @pl.when(middle & (col == 12))
+            def _():
+                pl.semaphore_signal(go, inc=1, device_id=(row, col + 3), device_id_type=MESH)
+
+            @pl.when(middle & (col == 19))
+            def _():
+                pl.semaphore_signal(go, inc=1, device_id=(row, col - 3), device_id_type=MESH)
+
         smooth_chunk(j)
         if turn == 0:
             pl.semaphore_wait(barrier, PLANE + GROUP)
@@ -172,12 +182,30 @@
 
         pack_chunk(j)
 
-        @pl.when(col < 31)
+        @pl.when((col < 31) & (col != 15))
         def _(j=j):
             to_right(j).start()
 
-        @pl.when(col > 0)
+        @pl.when((col > 0) & (col != 16))
         def _(j=j):
+            to_left(j).start()
+
+    @pl.when(crossing)
+    def _():
+        pl.semaphore_wait(go, 1)
+
+    @pl.when(middle & crossing)
+    def _():
+        pl.semaphore_signal(go, inc=1, device_id=((row - 1) * 3, col), device_id_type=MESH)
+
+    @pl.when(col == 15)
+    def _():
+        for j in order:
+            to_right(j).start()
+
+    @pl.when(col == 16)
+    def _():
+        for j in order:
             to_left(j).start()
 
     for j in order:
@@ -344,6 +372,7 @@
             pltpu.VMEM((GROUP, 8, 2, 8, 128), f32),
             pltpu.VMEM((PLANE, 2, 8, 128), f32),
             pltpu.VMEM((PLANE, 2, 8, 128), f32),
+            pltpu.SemaphoreType.REGULAR,
             dma, dma((2,)), dma((2,)), dma((2, 4)), dma((2, 4)),
             dma((PLANE,)), dma((PLANE,)), dma((GROUP,)), dma((GROUP,)), dma((PLANE,)), dma((PLANE,)),
         ],

time: 131 us -> 124 us (0.947)
  Pallas kernels: 130 us -> 123 us
    pallas_call x1, Pallas kernels: 111 us -> 104 us  [front(): pl.pallas_call(front_kernel, out_shape=(pltpu.VMEM((256, 256, 128), bf),...]
where the time goes in v6:
time: 124 us
  Pallas kernels  123 us (99%)
    pallas_call x1, Pallas kernels, front(): pl.pallas_call(front_kernel, out_shape=(pltpu.VMEM((256, 256, 128), bf),...  104 us
    pallas_call x1, Pallas kernels, back(): pl.pallas_call(back_kernel, out_shape=jax.ShapeDtypeStruct((128, 256, 128...  18.9 us

profile of v6, /device:TPU:1, one launch (start us, length us, event | category | flops | bytes accessed | tf_op | source)
XLA Modules:
  0.0 123.8 jit_solution(6621016986246194432)
XLA Ops:
  0.0 0.0 copy-start.1
  0.0 0.0 copy-start
  0.7 104.0 %front.1 = (bf16[256,256,128]{2,1,0:T(8,128)(2,1)S(1)}, f32[2,128,128]{2,1,0:T(8,128)S(1)}) custom-call(s32[2]{0:T(128)} %widths_ref.1, s32[1,1]{1,0:T(1,128)S(6)} %copy.6.region_ref, bf16[128,256,128]{2,1,0:T(8,128)(2,1)} %sky_ref.1), custom_call_target="tpu_custom_call" | custom-call | tf_op jit(solution)/shard_map/front/pallas_call | solution.py:351
  104.7 0.0 copy-done.1
  104.7 0.0 copy-done
  104.8 18.9 %back.1 = bf16[128,256,128]{2,1,0:T(8,128)(2,1)} custom-call(s32[1,1]{1,0:T(1,128)S(6)} %copy.6.region_ref, s32[8]{0:T(128)S(1)} %copy-done.1, f32[2,128,128]{2,1,0:T(8,128)S(1)} %get-tuple-element.7.gram_ref, f32[2,128]{1,0:T(2,128)S(1)} %copy-done, bf16[256,256,128]{2,1,0:T(8,128)(2,1)S(1)} %get-tuple-element.8.bands_ref), custom_call_target="tpu_custom_call" | custom-call | tf_op jit(solution)/shard_map/back/pallas_call | solution.py:506
Async XLA Ops:
  0.0 104.7 %copy-start.1 = (s32[8]{0:T(128)S(1)}, s32[8]{0:T(128)}, u32[]{:S(2)}) copy-start(s32[8]{0:T(128)} %rank_ref.1) | copy-start | bytes 100
  0.0 104.7 %copy-start = (f32[2,128]{1,0:T(2,128)S(1)}, f32[2,128]{1,0:T(2,128)}, u32[]{:S(2)}) copy-start(f32[2,128]{1,0:T(2,128)} %prior_ref.1) | copy-start | bytes 3076

commit v7 on v4

--- a/solution.py
+++ b/solution.py
@@ -371,6 +371,9 @@
     )(widths, region, sky)
 
 
+WIDE = 4
+
+
 def weights_of(grams, priors, cheb_t, keep):
     lanes = lax.broadcasted_iota(jnp.int32, (8, 128), 1)
     subs = lax.broadcasted_iota(jnp.int32, (8, 128), 0)
@@ -383,16 +386,35 @@
             blocks.append(block / 524288.0 + diag)
         blocks.append(cheb_t)
         mats.append(blocks)
-    for k in range(128):
+    for k in range(0, 128, WIDE):
         at, off = k // 8, k % 8
-        hit = lanes[0:1, :] == k
         for band in range(2):
             m = mats[band]
-            cols = [jnp.broadcast_to(b[:, k:k + 1], (8, 128)) for b in m]
-            inv = 1.0 / cols[at][off:off + 1, :]
-            line = m[at][off:off + 1, :] * inv
-            line = jnp.where(hit, 1.0 - inv, line)
-            mats[band] = [b - c * line for b, c in zip(m, cols)]
+            cols = [[jnp.broadcast_to(b[:, k + p:k + p + 1], (8, 128)) for b in m] for p in range(WIDE)]
+            hit = (lanes >= k) & (lanes < k + WIDE)
+            rows = [jnp.where(hit[0:1], jnp.where(lanes[0:1] == k + i, -1.0, 0.0), m[at][off + i:off + i + 1, :])
+                    for i in range(WIDE)]
+            d = [[cols[p][at][off + i:off + i + 1, :] for p in range(WIDE)] for i in range(WIDE)]
+            inv = []
+            for i in range(WIDE):
+                inv.append(1.0 / d[i][i])
+                for l in range(i + 1, WIDE):
+                    t = d[l][i] * inv[i]
+                    rows[l] = rows[l] - t * rows[i]
+                    for j in range(i + 1, WIDE):
+                        d[l][j] = d[l][j] - t * d[i][j]
+            for i in reversed(range(WIDE)):
+                line = rows[i]
+                for j in range(i + 1, WIDE):
+                    line = line - d[i][j] * rows[j]
+                rows[i] = line * inv[i]
+            fresh = []
+            for index, b in enumerate(m):
+                b = jnp.where(hit, 0.0, b)
+                for p in range(WIDE):
+                    b = b - cols[p][index] * rows[p]
+                fresh.append(b)
+            mats[band] = fresh
     out = []
     for band in range(2):
         mixed = mats[band][16] * keep

time: 126 us -> 121 us (0.960)
  Pallas kernels: 124 us -> 120 us
    pallas_call x1, Pallas kernels: 23.4 us -> 18.9 us  [back(): pl.pallas_call(back_kernel, out_shape=jax.ShapeDtypeStruct((128, 256, 128...]
where the time goes in v7:
time: 121 us
  Pallas kernels  120 us (99%)
    pallas_call x1, Pallas kernels, front(): pl.pallas_call(front_kernel, out_shape=(pltpu.VMEM((256, 256, 128), bf),...  101 us
    pallas_call x1, Pallas kernels, back(): pl.pallas_call(back_kernel, out_shape=jax.ShapeDtypeStruct((128, 256, 128...  18.9 us

profile of v7, /device:TPU:1, one launch (start us, length us, event | category | flops | bytes accessed | tf_op | source)
XLA Modules:
  0.0 120.8 jit_solution(3129831987771191907)
XLA Ops:
  0.0 0.0 copy-start.1
  0.0 0.0 copy-start
  0.7 101.1 %front.1 = (bf16[256,256,128]{2,1,0:T(8,128)(2,1)S(1)}, f32[2,128,128]{2,1,0:T(8,128)S(1)}) custom-call(s32[2]{0:T(128)} %widths_ref.1, s32[1,1]{1,0:T(1,128)S(6)} %copy.6.region_ref, bf16[128,256,128]{2,1,0:T(8,128)(2,1)} %sky_ref.1), custom_call_target="tpu_custom_call" | custom-call | tf_op jit(solution)/shard_map/front/pallas_call | solution.py:340
  101.8 0.0 copy-done.1
  101.8 0.0 copy-done
  101.8 18.9 %back.1 = bf16[128,256,128]{2,1,0:T(8,128)(2,1)} custom-call(s32[1,1]{1,0:T(1,128)S(6)} %copy.6.region_ref, s32[8]{0:T(128)S(1)} %copy-done.1, f32[2,128,128]{2,1,0:T(8,128)S(1)} %get-tuple-element.7.gram_ref, f32[2,128]{1,0:T(2,128)S(1)} %copy-done, bf16[256,256,128]{2,1,0:T(8,128)(2,1)S(1)} %get-tuple-element.8.bands_ref), custom_call_target="tpu_custom_call" | custom-call | tf_op jit(solution)/shard_map/back/pallas_call | solution.py:495
Async XLA Ops:
  0.0 101.8 %copy-start.1 = (s32[8]{0:T(128)S(1)}, s32[8]{0:T(128)}, u32[]{:S(2)}) copy-start(s32[8]{0:T(128)} %rank_ref.1) | copy-start | bytes 100
  0.0 101.8 %copy-start = (f32[2,128]{1,0:T(2,128)S(1)}, f32[2,128]{1,0:T(2,128)}, u32[]{:S(2)}) copy-start(f32[2,128]{1,0:T(2,128)} %prior_ref.1) | copy-start | bytes 3076

commit v8 on v7

--- a/solution.py
+++ b/solution.py
@@ -136,6 +136,16 @@
 
         lax.fori_loop(0, 4, pack_some, 0)
 
+    pl.semaphore_wait(barrier, PLANE + GROUP)
+
+    @pl.when(row < 3)
+    def _():
+        to_next.start()
+
+    @pl.when(row > 0)
+    def _():
+        to_last.start()
+
     load.wait()
     for j in ORDER:
         if j == ORDER[2]:
@@ -175,17 +185,6 @@
                 to_left(ORDER[1]).start()
 
         smooth_chunk(j)
-        if j == ORDER[0]:
-            pl.semaphore_wait(barrier, PLANE + GROUP)
-
-            @pl.when(row < 3)
-            def _():
-                to_next.start()
-
-            @pl.when(row > 0)
-            def _():
-                to_last.start()
-
         pack_chunk(j)
         late = j != ORDER[1]
 

time: 121 us -> 119 us (0.983)
  Pallas kernels: 120 us -> 118 us
    pallas_call x1, Pallas kernels: 101 us -> 99.3 us  [front(): pl.pallas_call(front_kernel, out_shape=(pltpu.VMEM((256, 256, 128), bf),...]
where the time goes in v8:
time: 119 us
  Pallas kernels  118 us (99%)
    pallas_call x1, Pallas kernels, front(): pl.pallas_call(front_kernel, out_shape=(pltpu.VMEM((256, 256, 128), bf),...  99.3 us
    pallas_call x1, Pallas kernels, back(): pl.pallas_call(back_kernel, out_shape=jax.ShapeDtypeStruct((128, 256, 128...  18.9 us

profile of v8, /device:TPU:1, one launch (start us, length us, event | category | flops | bytes accessed | tf_op | source)
XLA Modules:
  0.0 119.0 jit_solution(4474583115704823816)
XLA Ops:
  0.0 0.0 copy-start.1
  0.0 0.0 copy-start
  0.7 99.3 %front.1 = (bf16[256,256,128]{2,1,0:T(8,128)(2,1)S(1)}, f32[2,128,128]{2,1,0:T(8,128)S(1)}) custom-call(s32[2]{0:T(128)} %widths_ref.1, s32[1,1]{1,0:T(1,128)S(6)} %copy.6.region_ref, bf16[128,256,128]{2,1,0:T(8,128)(2,1)} %sky_ref.1), custom_call_target="tpu_custom_call" | custom-call | tf_op jit(solution)/shard_map/front/pallas_call | solution.py:339
  99.9 0.0 copy-done.1
  100.0 0.0 copy-done
  100.0 18.9 %back.1 = bf16[128,256,128]{2,1,0:T(8,128)(2,1)} custom-call(s32[1,1]{1,0:T(1,128)S(6)} %copy.6.region_ref, s32[8]{0:T(128)S(1)} %copy-done.1, f32[2,128,128]{2,1,0:T(8,128)S(1)} %get-tuple-element.7.gram_ref, f32[2,128]{1,0:T(2,128)S(1)} %copy-done, bf16[256,256,128]{2,1,0:T(8,128)(2,1)S(1)} %get-tuple-element.8.bands_ref), custom_call_target="tpu_custom_call" | custom-call | tf_op jit(solution)/shard_map/back/pallas_call | solution.py:494
Async XLA Ops:
  0.0 100.0 %copy-start.1 = (s32[8]{0:T(128)S(1)}, s32[8]{0:T(128)}, u32[]{:S(2)}) copy-start(s32[8]{0:T(128)} %rank_ref.1) | copy-start | bytes 100
  0.0 100.0 %copy-start = (f32[2,128]{1,0:T(2,128)S(1)}, f32[2,128]{1,0:T(2,128)}, u32[]{:S(2)}) copy-start(f32[2,128]{1,0:T(2,128)} %prior_ref.1) | copy-start | bytes 3076
